TPU v7x, 32 devices: a whole 2x2x4 slice. The times are simulated.
32 devices in a mesh: wide: 8 (over z, x), narrow: 4 (over y, core).
Axes of the slice: x: 2, y: 2, z: 4, core: 2. Of those that a mesh axis runs over, the one named last changes fastest.
Arguments:
- displacement: float32 [3, 3, 128, 128, 384], P(None, None, 'wide', 'narrow'), may hold values from -6 to 6
- material: int32 [128, 128, 24], P('wide', 'narrow'), may hold values 0 or 1
- level_set: float32 [384, 128, 128], P('wide', 'narrow'), may hold values from -6 to 6
Outputs:
- level_next: float32 [384, 128, 128], P('wide', 'narrow')
- speed: float32 [384, 128, 128], P('wide', 'narrow')
All inputs are finite; a program needn't handle non-finite values. No bound on the sum of `material` on one device may be relied on, other than what follows from the above.
Results may differ from a plain program's by a relative error of at most 0.00002.
Values sent between devices are 32-bit elements; how exact they have to be, the bound alone decides.
A program may use at most 192 MiB of HBM per device.

v0:
```python
import functools

import jax
import jax.numpy as jnp
from jax import lax
from jax.experimental import pallas as pl
from jax.experimental.pallas import tpu as pltpu
from jax.sharding import PartitionSpec as P

BZ = 16
EXT_PASSES = 4
HJ_STEPS = 3


SHEAR = 0.384615
LAME = 0.576923
WENO_EPS = 1e-06
TIME_STEP = 0.3
VAL_TAPS = (1.0 / 48.0, 23.0 / 48.0, 23.0 / 48.0, 1.0 / 48.0)
DER_TAPS = (-1.0 / 8.0, -5.0 / 8.0, 5.0 / 8.0, 1.0 / 8.0)


def shift_from(block, axis, dim, width, up):
    count = lax.axis_size(axis)
    if up:
        pairs = [(i, i + 1) for i in range(count - 1)]
        part = lax.slice_in_dim(block, block.shape[dim] - width, None, axis=dim)
    else:
        pairs = [(i + 1, i) for i in range(count - 1)]
        part = lax.slice_in_dim(block, 0, width, axis=dim)
    return lax.ppermute(part, axis, pairs)


def z_filters(u):
    size = u.shape[-1]
    lane = lax.broadcasted_iota(jnp.int32, u.shape, u.ndim - 1)
    last = u.ndim - 1
    before = jnp.where(lane == 0, 0.0, pltpu.roll(u, 1, last))
    after = jnp.where(lane == size - 1, 0.0, pltpu.roll(u, size - 1, last))
    second = jnp.where(lane >= size - 2, 0.0, pltpu.roll(u, size - 2, last))
    val = VAL_TAPS[0] * (before + second) + VAL_TAPS[1] * (u + after)
    der = DER_TAPS[3] * (second - before) + DER_TAPS[2] * (after - u)
    return val, der


def energy_kernel(own_ref, xh_ref, yh_ref, stiff_ref, out_ref, peak_ref, val_ref, der_ref):
    load = pl.program_id(0)
    size_x, size_y, size_z = own_ref.shape[2:]
    rows = val_ref.shape[2]

    def plane(c, p, body, tail):
        val, der = z_filters(body)
        val_ref[c, p, 0:size_y, :] = val
        der_ref[c, p, 0:size_y, :] = der
        val, der = z_filters(tail)
        val_ref[c, p, size_y:rows, :] = val
        der_ref[c, p, size_y:rows, :] = der

    for c in range(3):
        @pl.loop(0, size_x)
        def _(p):
            plane(c, p, own_ref[0, c, p], yh_ref[0, c, p])

        @pl.loop(0, 3)
        def _(q):
            plane(c, size_x + q, xh_ref[0, c, q], yh_ref[0, c, size_x + q])

    def taps_x(ref, c, idx, cols):
        parts = [ref[c, i, :, cols] for i in idx]
        return parts[0] + parts[3], parts[1] + parts[2], parts[3] - parts[0], parts[2] - parts[1]

    def along_y(val_part, der_part):
        total = None
        for k, shift in enumerate((1, 0, rows - 1, rows - 2)):
            term = None
            if val_part is not None:
                term = VAL_TAPS[k] * val_part
            if der_part is not None:
                extra = DER_TAPS[k] * der_part
                term = extra if term is None else term + extra
            if shift:
                term = pltpu.roll(term, shift, 0)
            total = term if total is None else total + term
        return total[0:size_y]

    chunk = 128

    @pl.loop(0, size_x)
    def _(p):
        low = jnp.where(p == 0, size_x + 2, p - 1)
        idx = (low, p, p + 1, p + 2)
        for piece in range(size_z // chunk):
            cols = pl.ds(piece * chunk, chunk)
            fields = []
            for c in range(3):
                outer, inner, far, near = taps_x(val_ref, c, idx, cols)
                vv = VAL_TAPS[0] * outer + VAL_TAPS[1] * inner
                dv = DER_TAPS[3] * far + DER_TAPS[2] * near
                outer, inner, _, _ = taps_x(der_ref, c, idx, cols)
                vz = VAL_TAPS[0] * outer + VAL_TAPS[1] * inner
                fields.append((vv, dv, vz))
            exx = along_y(fields[0][1], None)
            eyy = along_y(None, fields[1][0])
            ezz = along_y(fields[2][2], None)
            exy = 0.5 * along_y(fields[1][1], fields[0][0])
            exz = 0.5 * along_y(fields[0][2] + fields[2][1], None)
            eyz = 0.5 * along_y(fields[1][2], fields[2][0])
            trace = exx + eyy + ezz
            square = exx * exx + eyy * eyy + ezz * ezz + 2.0 * (exy * exy + exz * exz + eyz * eyz)
            density = SHEAR * square + 0.5 * LAME * trace * trace

            @pl.when(load == 0)
            def _():
                out_ref[p, :, cols] = density

            @pl.when(load > 0)
            def _():
                out_ref[p, :, cols] = out_ref[p, :, cols] + density

    @pl.when(load == pl.num_programs(0) - 1)
    def _():
        peak_ref[...] = jnp.zeros(peak_ref.shape, jnp.float32)

        @pl.loop(0, size_x)
        def _(p):
            energy = stiff_ref[p] * out_ref[p]
            out_ref[p] = energy
            peak_ref[...] = jnp.maximum(peak_ref[...], energy)


def slab_energy(displacement, material, early):
    loads, comps, size_x, size_y, size_z = displacement.shape
    low_y = shift_from(displacement, "narrow", 3, 1, True)
    high_y = shift_from(displacement, "narrow", 3, 2, False)
    filler = jnp.zeros((loads, comps, size_x, 5, size_z), jnp.float32)
    tail = jnp.concatenate([high_y, filler, low_y], axis=3)
    ends = jnp.concatenate(
        [
            jnp.concatenate([displacement[:, :, :2], displacement[:, :, -1:]], axis=2),
            jnp.concatenate([tail[:, :, :2], tail[:, :, -1:]], axis=2),
        ],
        axis=3,
    )
    high_x = shift_from(ends, "wide", 2, 2, False)
    low_x = shift_from(ends, "wide", 2, 1, True)
    beside = jnp.concatenate([high_x, low_x], axis=2)
    beside_own = beside[:, :, :, :size_y]
    tail = jnp.concatenate([tail, beside[:, :, :, size_y:]], axis=2)
    stiffness = 0.2 + 0.8 * jnp.repeat(material.astype(jnp.float32), BZ, axis=2)
    beside_own, tail, early = lax.optimization_barrier((beside_own, tail, early))
    planes = size_x + 3
    rows = size_y + 8
    energy, peak = pl.pallas_call(
        energy_kernel,
        grid=(loads,),
        out_shape=(
            jax.ShapeDtypeStruct((size_x, size_y, size_z), jnp.float32),
            jax.ShapeDtypeStruct((size_y, size_z), jnp.float32),
        ),
        in_specs=[
            pl.BlockSpec((1, comps, size_x, size_y, size_z), lambda i: (i, 0, 0, 0, 0)),
            pl.BlockSpec((1, comps, 3, size_y, size_z), lambda i: (i, 0, 0, 0, 0)),
            pl.BlockSpec((1, comps, planes, 8, size_z), lambda i: (i, 0, 0, 0, 0)),
            pl.BlockSpec((size_x, size_y, size_z), lambda i: (0, 0, 0)),
        ],
        out_specs=(
            pl.BlockSpec((size_x, size_y, size_z), lambda i: (0, 0, 0)),
            pl.BlockSpec((size_y, size_z), lambda i: (0, 0)),
        ),
        scratch_shapes=[
            pltpu.VMEM((comps, planes, rows, size_z), jnp.float32),
            pltpu.VMEM((comps, planes, rows, size_z), jnp.float32),
        ],
        compiler_params=pltpu.CompilerParams(vmem_limit_bytes=40 << 20),
        cost_estimate=pl.CostEstimate(flops=100000000, bytes_accessed=12000000, transcendentals=0),
    )(displacement, beside_own, tail, stiffness)
    return energy, jnp.max(peak), early


def weno_pair(d):
    e = [d[k + 1] - d[k] for k in range(5)]
    s = [e[k + 1] - e[k] for k in range(4)]
    bend = [(13.0 / 12.0) * s[k] * s[k] for k in range(4)]
    twice = [None] + [2.0 * e[k] for k in (1, 2, 3)]
    sixth = [None] + [(1.0 / 6.0) * e[k] for k in (1, 2, 3)]
    third = (1.0 / 3.0) * e[2]

    def blend(base, b_one, t_one, b_two, t_two, b_three, t_three, r_one, r_two, r_three):
        a = WENO_EPS + b_one + 0.25 * t_one * t_one
        b = WENO_EPS + b_two + 0.25 * t_two * t_two
        c = WENO_EPS + b_three + 0.25 * t_three * t_three
        a = a * a
        b = b * b
        c = c * c
        w_one = 0.1 * (b * c)
        w_two = 0.6 * (a * c)
        w_three = 0.3 * (a * b)
        return base + (w_one * r_one + w_two * r_two + w_three * r_three) / (w_one + w_two + w_three)

    minus = blend(
        d[2],
        bend[0], s[0] + twice[1],
        bend[1], e[1] + e[2],
        bend[2], s[2] - twice[2],
        (5.0 / 6.0) * e[1] - (1.0 / 3.0) * e[0],
        sixth[1] + third,
        2.0 * third - sixth[3],
    )
    plus = blend(
        d[3],
        bend[3], s[3] - twice[3],
        bend[2], e[2] + e[3],
        bend[1], s[1] + twice[2],
        (1.0 / 3.0) * e[4] - (5.0 / 6.0) * e[3],
        -(sixth[3] + third),
        sixth[1] - 2.0 * third,
    )
    return minus, plus


def lane_shift(u, offset, ghost):
    if offset == 0:
        return u
    size = u.shape[-1]
    lane = lax.broadcasted_iota(jnp.int32, u.shape, u.ndim - 1)
    moved = pltpu.roll(u, (-offset) % size, u.ndim - 1)
    outside = lane >= size - offset if offset > 0 else lane < -offset
    return jnp.where(outside, ghost, moved)


MARGIN = 3 * (HJ_STEPS - 1) + EXT_PASSES
SIDE = -(-MARGIN // 8) * 8 + 8


CHUNK = 8


def march_kernel(
    place, peak, vel_own, vel_low, vel_high, phi_own, phi_low, phi_high,
    next_ref, speed_ref, pull, keep, one, two, first, second,
):
    deep, rows, size_x = pull.shape
    own_y = rows - 2 * SIDE
    own_z = deep - 2 * MARGIN
    scale = peak[0] + 1e-06

    def settle(z, lo, values, ghost):
        here = place[0] + z
        shape = values.shape
        row = lax.broadcasted_iota(jnp.int32, shape, 0) + (lo + place[2])
        lowest = jnp.where((here >= 0) & (here < place[1]), 0, place[3])
        return jnp.where((row >= lowest) & (row < place[3]), values, ghost)

    def window(margin):
        lo = (SIDE - margin) // 8 * 8
        return lo, rows - lo

    @pl.loop(0, deep)
    def _(z):
        def fill(lo, size, energy, phi):
            at = pl.ds(lo, size)
            velocity = energy / scale - 0.5
            weight = 1.0 / (1.0 + 4.0 * phi * phi)
            pull[z, at, :] = weight * velocity
            keep[z, at, :] = (1.0 - weight) * (1.0 / 6.0)
            one[z, at, :] = settle(z, lo, velocity, 0.0)
            first[z, at, :] = settle(z, lo, phi, 1.0)

        fill(SIDE - MARGIN, MARGIN, vel_low[z], phi_low[z])
        fill(SIDE, own_y, vel_own[z], phi_own[z])
        fill(SIDE + own_y, MARGIN, vel_high[z], phi_high[z])

    source, target = one, two
    for step in range(EXT_PASSES):
        margin = MARGIN - 1 - step
        lo, hi = window(margin)

        def extend(z, source=source, target=target, lo=lo, hi=hi):
            for start in range(lo, hi, 16):
                at = pl.ds(start, 16)
                mid = source[z, at, :]
                total = source[z - 1, at, :] + source[z + 1, at, :]
                total = total + (source[z, pl.ds(start - 1, 16), :] + source[z, pl.ds(start + 1, 16), :])
                total = total + (lane_shift(mid, 1, 0.0) + lane_shift(mid, -1, 0.0))
                value = pull[z, at, :] + keep[z, at, :] * total
                target[z, at, :] = settle(z, start, value, 0.0)

        pl.loop(step + 1, deep - step - 1)(extend)
        source, target = target, source
    speed = source

    source, target = first, second
    for step in range(HJ_STEPS):
        margin = 3 * (HJ_STEPS - 1 - step)
        lo, hi = window(margin)
        final = step == HJ_STEPS - 1

        def march(z, source=source, target=target, lo=lo, hi=hi, final=final):
            for start in range(lo, hi, CHUNK):
                at = pl.ds(start, CHUNK)
                mid = source[z, at, :]
                lines = (
                    [source[z + k, at, :] for k in range(-3, 4)],
                    [source[z, pl.ds(start + k, CHUNK), :] for k in range(-3, 4)],
                    [lane_shift(mid, k, 1.0) for k in range(-3, 4)],
                )
                grow_plus = None
                grow_minus = None
                for line in lines:
                    minus, plus = weno_pair([line[k + 1] - line[k] for k in range(6)])
                    up = jnp.maximum(jnp.maximum(minus, 0.0), -jnp.minimum(plus, 0.0))
                    down = jnp.maximum(-jnp.minimum(minus, 0.0), jnp.maximum(plus, 0.0))
                    grow_plus = up * up if grow_plus is None else grow_plus + up * up
                    grow_minus = down * down if grow_minus is None else grow_minus + down * down
                rate = speed[z, at, :]
                growth = jnp.sqrt(jnp.where(rate > 0.0, grow_plus, grow_minus))
                value = mid - TIME_STEP * (rate * growth)
                if final:
                    next_ref[z - MARGIN, pl.ds(start - SIDE, CHUNK), :] = value
                    speed_ref[z - MARGIN, pl.ds(start - SIDE, CHUNK), :] = rate
                else:
                    target[z, at, :] = settle(z, start, value, 1.0)

        pl.loop(MARGIN - margin, MARGIN + own_z + margin)(march)
        source, target = target, source


def rows_beside(block, width):
    low = shift_from(block, "narrow", 1, width, True)
    high = shift_from(block, "narrow", 1, width, False)
    return block, low, high


def march(velocity, phi, peak, own_z, own_y):
    deep, _, size_x = phi[0].shape
    place = jnp.stack(
        [
            lax.axis_index("wide") * own_z - MARGIN,
            lax.axis_size("wide") * own_z,
            lax.axis_index("narrow") * own_y - SIDE,
            lax.axis_size("narrow") * own_y,
        ]
    ).astype(jnp.int32)
    result = jax.ShapeDtypeStruct((own_z, own_y, size_x), jnp.float32)
    smem = pl.BlockSpec(memory_space=pltpu.SMEM)
    vmem = pl.BlockSpec(memory_space=pltpu.VMEM)
    return pl.pallas_call(
        march_kernel,
        out_shape=(result, result),
        in_specs=[smem, smem] + [vmem] * 6,
        out_specs=(vmem, vmem),
        scratch_shapes=[pltpu.VMEM((deep, own_y + 2 * SIDE, size_x), jnp.float32)] * 6,
        compiler_params=pltpu.CompilerParams(vmem_limit_bytes=56 << 20),
        cost_estimate=pl.CostEstimate(flops=200000000, bytes_accessed=8000000, transcendentals=0),
    )(place, jnp.reshape(peak, (1,)), *velocity, *phi)


def per_device(displacement, material, level_set):
    own_z, own_y, size_x = level_set.shape
    low = shift_from(level_set, "wide", 0, MARGIN, True)
    high = shift_from(level_set, "wide", 0, MARGIN, False)
    phi = rows_beside(jnp.concatenate([low, level_set, high], axis=0), MARGIN)
    energy, own_peak, phi = slab_energy(displacement, material, phi)
    devices = lax.axis_size("wide") * lax.axis_size("narrow")
    peaks = lax.all_to_all(
        jnp.full((devices, 1, 128), own_peak), ("wide", "narrow"), split_axis=0, concat_axis=0, tiled=True
    )
    flipped = jnp.pad(jnp.transpose(energy, (2, 1, 0)), ((MARGIN, MARGIN), (0, 0), (0, 0)))
    chunks = [
        lax.slice_in_dim(flipped, k * own_z, k * own_z + own_z + 2 * MARGIN, axis=0)
        for k in range(lax.axis_size("wide"))
    ]
    moved = lax.all_to_all(
        jnp.concatenate(chunks, axis=0), "wide", split_axis=0, concat_axis=2, tiled=True
    )
    return march(rows_beside(moved, MARGIN), phi, jnp.max(peaks), own_z, own_y)


def solution(mesh):
    return jax.shard_map(
        per_device,
        mesh=mesh,
        in_specs=(
            P(None, None, "wide", "narrow", None),
            P("wide", "narrow", None),
            P("wide", "narrow", None),
        ),
        out_specs=(P("wide", "narrow", None), P("wide", "narrow", None)),
        check_vma=False,
    )
```

profile of v0, /device:TPU:17, one launch (start us, length us, event | category | flops | bytes accessed | tf_op | source)
XLA Modules:
  0.0 258.9 jit_solution(16829662235163998107)
XLA Ops:
  0.6 1.6 slice.80
  2.2 2.6 collective-permute-start
  4.8 1.7 slice.81
  6.5 3.0 %collective-permute-start.1 = (f32[3,3,16,1,384]{4,3,2,1,0:T(1,128)S(1)}, f32[3,3,16,1,384]{4,3,2,1,0:T(1,128)S(1)}, u32[]{:S(2)}, u32[]{:S(2)}) collective-permute-start(f32[3,3,16,1,384]{4,3,2,1,0:T(1,128)S(1)} %slice.81), channel_id=1, source_target_pairs={{0,1},{1,2},{2,3},{4,5},{5,6},{6,7},{8,9},{9,10},{10,11},{12,13},{... | collective-permute-start | bytes 663560 | tf_op jit(solution)/shard_map/ppermute | solution.py:31
  9.5 0.0 slice-start.2
  9.6 2.8 %collective-permute-done.1 = f32[3,3,16,1,384]{4,3,2,1,0:T(1,128)S(1)} collective-permute-done((f32[3,3,16,1,384]{4,3,2,1,0:T(1,128)S(1)}, f32[3,3,16,1,384]{4,3,2,1,0:T(1,128)S(1)}, u32[]{:S(2)}, u32[]{:S(2)}) %collective-permute-start.1) | collective-permute-done | bytes 221216 | tf_op jit(solution)/shard_map/ppermute | solution.py:31
  12.4 0.1 broadcast_in_dim.9
  12.6 0.2 fusion.1
  12.8 0.3 copy-done.3
  13.1 1.2 copy-done
  14.3 1.1 slice.102
  15.4 3.0 %collective-permute-start.2 = (f32[3,3,2,40,384]{4,3,2,1,0:T(8,128)}, f32[3,3,2,40,384]{4,3,2,1,0:T(8,128)}, u32[]{:S(2)}, u32[]{:S(2)}) collective-permute-start(f32[3,3,2,40,384]{4,3,2,1,0:T(8,128)} %slice.102), channel_id=1, source_target_pairs={{4,0},{8,4},{12,8},{16,12},{20,16},{24,20},{28,24},{5,1},{9,5},{13... | collective-permute-start | bytes 3317768 | tf_op jit(solution)/shard_map/ppermute | solution.py:31
  18.4 1.0 fusion.4
  19.4 2.3 collective-permute-start.4
  21.7 3.9 %collective-permute-start.5 = (f32[10,32,128]{2,1,0:T(8,128)S(1)}, f32[10,32,128]{2,1,0:T(8,128)S(1)}, u32[]{:S(2)}, u32[]{:S(2)}) collective-permute-start(f32[10,32,128]{2,1,0:T(8,128)S(1)} %get-tuple-element.28), channel_id=1, source_target_pairs={{4,0},{8,4},{12,8},{16,12},{20,16},{24,20},{28,24},{5,1},{9,5},{13... | collective-permute-start | bytes 491528 | tf_op jit(solution)/shard_map/ppermute | solution.py:31
  25.6 1.9 broadcast_in_dim.10
  27.5 2.3 copy.38.stiff_ref
  29.8 0.0 copy-start.2
  29.8 19.1 %collective-permute-done.4 = f32[10,32,128]{2,1,0:T(8,128)} collective-permute-done((f32[10,32,128]{2,1,0:T(8,128)S(1)}, f32[10,32,128]{2,1,0:T(8,128)}, u32[]{:S(2)}, u32[]{:S(2)}) %collective-permute-start.4) | collective-permute-done | bytes 163872 | tf_op jit(solution)/shard_map/ppermute | solution.py:31
  49.0 0.9 constant_dynamic-update-slice_fusion.4
  49.9 1.1 slice.103
  51.0 4.0 %collective-permute-start.3 = (f32[3,3,1,40,384]{4,3,2,1,0:T(8,128)S(1)}, f32[3,3,1,40,384]{4,3,2,1,0:T(8,128)S(1)}, u32[]{:S(2)}, u32[]{:S(2)}) collective-permute-start(f32[3,3,1,40,384]{4,3,2,1,0:T(8,128)S(1)} %slice.103), channel_id=1, source_target_pairs={{0,4},{4,8},{8,12},{12,16},{16,20},{20,24},{24,28},{1,5},{5,9},{9,... | collective-permute-start | bytes 1658888 | tf_op jit(solution)/shard_map/ppermute | solution.py:31
  55.0 0.1 constant_dynamic-update-slice_fusion.3
  55.1 0.0 slice-start
  55.1 0.1 fusion.3
  55.2 0.1 copy.36
  55.4 3.5 %collective-permute-start.6 = (f32[68,10,128]{2,0,1:T(8,128)S(1)}, f32[68,10,128]{2,0,1:T(8,128)S(1)}, u32[]{:S(2)}, u32[]{:S(2)}) collective-permute-start(f32[68,10,128]{2,0,1:T(8,128)S(1)} %copy.36), channel_id=1, source_target_pairs={{0,1},{1,2},{2,3},{4,5},{5,6},{6,7},{8,9},{9,10},{10,11},{12,13},{... | collective-permute-start | bytes 1044488 | tf_op jit(solution)/shard_map/ppermute | solution.py:31
  58.9 0.1 copy.37
  59.0 1.9 collective-permute-start.7
  60.9 1.3 constant_dynamic-update-slice_fusion.1
  62.3 5.4 %collective-permute-done.3 = f32[3,3,1,40,384]{4,3,2,1,0:T(8,128)S(1)} collective-permute-done((f32[3,3,1,40,384]{4,3,2,1,0:T(8,128)S(1)}, f32[3,3,1,40,384]{4,3,2,1,0:T(8,128)S(1)}, u32[]{:S(2)}, u32[]{:S(2)}) %collective-permute-start.3) | collective-permute-done | bytes 552992 | tf_op jit(solution)/shard_map/ppermute | solution.py:31
  67.7 0.0 copy-start.4
  67.7 0.0 slice-start.1
  67.8 0.2 slice.104.xh_ref
  67.9 0.7 copy-done.4
  68.7 0.6 pad_maximum_fusion.yh_ref
  69.3 0.4 slice-done.1
  69.6 36.6 %shard_map.50 = (f32[16,32,384]{2,1,0:T(8,128)S(1)}, f32[32,384]{1,0:T(8,128)S(1)}) custom-call(f32[3,3,16,32,384]{4,3,2,1,0:T(8,128)S(1)} %bitcast.13, f32[3,3,3,32,384]{4,3,2,1,0:T(8,128)S(1)} %slice.104.xh_ref, f32[3,3,19,8,384]{4,3,2,1,0:T(8,128)S(1)} %pad_maximum_fusion.yh_ref, f32[16,32,384]{2,1,0:T(8,128)S(1)} %copy.38.stiff_ref), custom_call_target="tpu_custom_call" | custom-call | flops 100000000 | bytes 12000000 | tf_op jit(solution)/shard_map/pallas_call | solution.py:153
  106.3 0.6 pad_slice_fusion
  106.9 1.0 concatenate.31
  107.8 2.9 %copy.40 = f32[544,32,16]{1,2,0:T(8,128)} copy(f32[544,32,16]{0,1,2:T(8,128)S(1)} %concatenate.31) | data formatting | bytes 2228224 | tf_op jit(solution)/shard_map/concatenate | solution.py:374
  110.8 4.1 %reshape.13 = f32[8,1,34816]{2,1,0:T(1,128)S(1)} reshape(f32[544,16,32]{2,1,0:T(8,128)} %bitcast.15) | data formatting | bytes 2228224
  114.8 29.8 %all_to_all.23 = f32[8,1,34816]{2,1,0:T(1,128)S(1)} all-to-all(f32[8,1,34816]{2,1,0:T(1,128)S(1)} %reshape.13), channel_id=1, replica_groups=mesh['wide'=8,'narrow'=4] {'wide'}, dimensions={0} | all-to-all | bytes 2228224 | tf_op jit(solution)/shard_map/all_to_all | solution.py:373
  144.6 0.5 broadcast.37
  145.2 3.3 %reduce = f32[8,34816]{1,0:T(8,128)S(1)} reduce(f32[8,1,34816]{2,1,0:T(1,128)S(1)} %all_to_all.23, f32[]{:T(128)} %broadcast.37), dimensions={1}, to_apply=%all_to_all.17.reduce_sub_computation | reduce | bytes 2228228 | tf_op jit(solution)/shard_map/all_to_all | solution.py:373
  148.5 3.5 %reshape.14 = f32[544,16,32]{2,1,0:T(8,128)} reshape(f32[8,34816]{1,0:T(8,128)S(1)} %reduce) | data formatting | bytes 2228224
  152.0 4.5 %copy.41 = f32[8,68,32,16]{1,3,0,2:T(8,128)S(1)} copy(f32[8,68,32,16]{2,3,1,0:T(8,128)} %bitcast.16) | data formatting | bytes 2228224 | tf_op jit(solution)/shard_map/all_to_all | solution.py:373
  156.4 0.9 fusion.2
  157.4 2.1 copy.42
  159.5 3.5 %collective-permute-start.8 = (f32[68,10,128]{2,0,1:T(8,128)}, f32[68,10,128]{2,0,1:T(8,128)}, u32[]{:S(2)}, u32[]{:S(2)}) collective-permute-start(f32[68,10,128]{2,0,1:T(8,128)} %copy.42), channel_id=1, source_target_pairs={{0,1},{1,2},{2,3},{4,5},{5,6},{6,7},{8,9},{9,10},{10,11},{12,13},{... | collective-permute-start | bytes 1044488 | tf_op jit(solution)/shard_map/ppermute | solution.py:31
  163.0 1.0 copy.43
  164.0 1.9 collective-permute-start.9
  165.9 0.6 reduce_max.18
  166.5 1.2 broadcast_in_dim.11
  167.7 5.2 %all-to-all-start = ((f32[32,1,128]{2,1,0:T(1,128)}), f32[32,1,128]{2,1,0:T(1,128)S(1)}, u32[]{:S(2)}, u32[]{:S(2)}) async-start(f32[32,1,128]{2,1,0:T(1,128)} %broadcast_in_dim.11), calls=%async_computation | async-start | bytes 32768 | tf_op jit(solution)/shard_map/all_to_all | solution.py:365
  172.9 0.7 pad_add_fusion.place
  173.6 0.9 copy.47.phi_low
  174.5 1.9 copy.48.phi_high
  176.4 1.2 all-to-all-done
  177.6 0.6 reduce_max.19
  178.2 1.7 copy.44.vel_own
  179.9 1.9 copy.45.vel_low
  181.8 0.9 copy.46.vel_high
  182.7 76.2 %shard_map.51 = (f32[48,32,128]{2,1,0:T(8,128)}, f32[48,32,128]{2,1,0:T(8,128)}) custom-call(s32[4]{0:T(128)} %pad_add_fusion.place, f32[1]{0:T(128)} %bitcast.4.peak, f32[68,32,128]{2,1,0:T(8,128)} %copy.44.vel_own, f32[68,10,128]{2,1,0:T(8,128)} %copy.45.vel_low, f32[68,10,128]{2,1,0:T(8,128)} %copy.46.vel_high, f32[68,32,128]{2,1,0:T(8,128)} %copy-done.1, ...), custom_call_target="tpu_custom_call" | custom-call | flops 200000000 | bytes 8000000 | tf_op jit(solution)/shard_map/pallas_call | solution.py:347
  (27 shorter events, 0.2 us)
Async XLA Ops:
  2.2 10.2 %collective-permute-start = (f32[3,3,16,2,384]{4,3,2,1,0:T(2,128)S(1)}, f32[3,3,16,2,384]{4,3,2,1,0:T(2,128)S(1)}, u32[]{:S(2)}, u32[]{:S(2)}) collective-permute-start(f32[3,3,16,2,384]{4,3,2,1,0:T(2,128)S(1)} %slice.80), channel_id=1, source_target_pairs={{1,0},{2,1},{3,2},{5,4},{6,5},{7,6},{9,8},{10,9},{11,10},{13,12},{... | collective-permute-start | bytes 1327112 | tf_op jit(solution)/shard_map/ppermute | solution.py:31
  6.5 5.9 %collective-permute-start.1 = (f32[3,3,16,1,384]{4,3,2,1,0:T(1,128)S(1)}, f32[3,3,16,1,384]{4,3,2,1,0:T(1,128)S(1)}, u32[]{:S(2)}, u32[]{:S(2)}) collective-permute-start(f32[3,3,16,1,384]{4,3,2,1,0:T(1,128)S(1)} %slice.81), channel_id=1, source_target_pairs={{0,1},{1,2},{2,3},{4,5},{5,6},{6,7},{8,9},{9,10},{10,11},{12,13},{... | collective-permute-start | bytes 663560 | tf_op jit(solution)/shard_map/ppermute | solution.py:31
  9.5 3.0 %slice-start.2 = ((f32[3,3,16,32,384]{4,3,2,1,0:T(8,128)}), f32[3,3,2,32,384]{4,3,2,1,0:T(8,128)S(1)}, s32[]{:S(2)}) async-start(f32[3,3,16,32,384]{4,3,2,1,0:T(8,128)} %own_ref.1), calls=%async_computation.4 | async-start | bytes 1769472 | tf_op jit(solution)/shard_map/slice | solution.py:139
  9.6 3.0 %slice-start.3 = ((f32[3,3,16,32,384]{4,3,2,1,0:T(8,128)}), f32[3,3,1,32,384]{4,3,2,1,0:T(8,128)S(1)}, s32[]{:S(2)}) async-start(f32[3,3,16,32,384]{4,3,2,1,0:T(8,128)} %own_ref.1), calls=%async_computation.5 | async-start | bytes 884736 | tf_op jit(solution)/shard_map/slice | solution.py:139
  12.4 0.7 copy-start.3
  13.1 1.2 copy-start
  14.3 11.3 %copy-start.7 = (s32[16,32,24]{1,2,0:T(8,128)S(1)}, s32[16,32,24]{1,2,0:T(8,128)}, u32[]{:S(2)}) copy-start(s32[16,32,24]{1,2,0:T(8,128)} %param.4) | copy-start | bytes 147460
  15.4 45.6 %collective-permute-start.2 = (f32[3,3,2,40,384]{4,3,2,1,0:T(8,128)}, f32[3,3,2,40,384]{4,3,2,1,0:T(8,128)}, u32[]{:S(2)}, u32[]{:S(2)}) collective-permute-start(f32[3,3,2,40,384]{4,3,2,1,0:T(8,128)} %slice.102), channel_id=1, source_target_pairs={{4,0},{8,4},{12,8},{16,12},{20,16},{24,20},{28,24},{5,1},{9,5},{13... | collective-permute-start | bytes 3317768 | tf_op jit(solution)/shard_map/ppermute | solution.py:31
  19.4 29.6 %collective-permute-start.4 = (f32[10,32,128]{2,1,0:T(8,128)S(1)}, f32[10,32,128]{2,1,0:T(8,128)}, u32[]{:S(2)}, u32[]{:S(2)}) collective-permute-start(f32[10,32,128]{2,1,0:T(8,128)S(1)} %get-tuple-element.29), channel_id=1, source_target_pairs={{0,4},{4,8},{8,12},{12,16},{16,20},{20,24},{24,28},{1,5},{5,9},{9,... | collective-permute-start | bytes 491528 | tf_op jit(solution)/shard_map/ppermute | solution.py:31
  21.7 33.4 %collective-permute-start.5 = (f32[10,32,128]{2,1,0:T(8,128)S(1)}, f32[10,32,128]{2,1,0:T(8,128)S(1)}, u32[]{:S(2)}, u32[]{:S(2)}) collective-permute-start(f32[10,32,128]{2,1,0:T(8,128)S(1)} %get-tuple-element.28), channel_id=1, source_target_pairs={{4,0},{8,4},{12,8},{16,12},{20,16},{24,20},{28,24},{5,1},{9,5},{13... | collective-permute-start | bytes 491528 | tf_op jit(solution)/shard_map/ppermute | solution.py:31
  29.8 25.2 %copy-start.2 = (f32[48,32,128]{2,1,0:T(8,128)S(1)}, f32[48,32,128]{2,1,0:T(8,128)}, u32[]{:S(2)}) copy-start(f32[48,32,128]{2,1,0:T(8,128)} %param.5) | copy-start | bytes 2359300
  51.0 16.7 %collective-permute-start.3 = (f32[3,3,1,40,384]{4,3,2,1,0:T(8,128)S(1)}, f32[3,3,1,40,384]{4,3,2,1,0:T(8,128)S(1)}, u32[]{:S(2)}, u32[]{:S(2)}) collective-permute-start(f32[3,3,1,40,384]{4,3,2,1,0:T(8,128)S(1)} %slice.103), channel_id=1, source_target_pairs={{0,4},{4,8},{8,12},{12,16},{16,20},{20,24},{24,28},{1,5},{5,9},{9,... | collective-permute-start | bytes 1658888 | tf_op jit(solution)/shard_map/ppermute | solution.py:31
  55.1 3.9 %copy-start.1 = (f32[68,32,128]{2,1,0:T(8,128)}, f32[68,32,128]{2,1,0:T(8,128)S(1)}, u32[]{:S(2)}) copy-start(f32[68,32,128]{2,1,0:T(8,128)S(1)} %constant_dynamic-update-slice_fusion.2.phi_own) | copy-start | bytes 3342340
  55.1 14.1 %slice-start = ((s8[7077888]{0:T(1024)(128)(4,1)}), s8[4194304]{0:T(1024)(128)(4,1)S(1)}, s32[]{:S(2)}) async-start(s8[7077888]{0:T(1024)(128)(4,1)} %bitcast.12), calls=%async_computation.2 | async-start | bytes 8388608
  55.4 13.9 %collective-permute-start.6 = (f32[68,10,128]{2,0,1:T(8,128)S(1)}, f32[68,10,128]{2,0,1:T(8,128)S(1)}, u32[]{:S(2)}, u32[]{:S(2)}) collective-permute-start(f32[68,10,128]{2,0,1:T(8,128)S(1)} %copy.36), channel_id=1, source_target_pairs={{0,1},{1,2},{2,3},{4,5},{5,6},{6,7},{8,9},{9,10},{10,11},{12,13},{... | collective-permute-start | bytes 1044488 | tf_op jit(solution)/shard_map/ppermute | solution.py:31
  59.0 10.3 %collective-permute-start.7 = (f32[68,10,128]{2,0,1:T(8,128)S(1)}, f32[68,10,128]{2,0,1:T(8,128)}, u32[]{:S(2)}, u32[]{:S(2)}) collective-permute-start(f32[68,10,128]{2,0,1:T(8,128)S(1)} %copy.37), channel_id=1, source_target_pairs={{1,0},{2,1},{3,2},{5,4},{6,5},{7,6},{9,8},{10,9},{11,10},{13,12},{... | collective-permute-start | bytes 1044488 | tf_op jit(solution)/shard_map/ppermute | solution.py:31
  67.7 0.9 copy-start.4
  67.7 1.9 slice-start.1
  69.3 37.0 %copy-start.5 = (f32[68,10,128]{2,0,1:T(8,128)}, f32[68,10,128]{2,0,1:T(8,128)S(1)}, u32[]{:S(2)}) copy-start(f32[68,10,128]{2,0,1:T(8,128)S(1)} %collective-permute-done.6) | copy-start | bytes 1044484
  157.4 16.2 %copy-start.6 = (f32[68,10,128]{2,0,1:T(8,128)S(1)}, f32[68,10,128]{2,0,1:T(8,128)}, u32[]{:S(2)}) copy-start(f32[68,10,128]{2,0,1:T(8,128)} %copy-done.5) | copy-start | bytes 1044484
  159.5 20.4 %collective-permute-start.8 = (f32[68,10,128]{2,0,1:T(8,128)}, f32[68,10,128]{2,0,1:T(8,128)}, u32[]{:S(2)}, u32[]{:S(2)}) collective-permute-start(f32[68,10,128]{2,0,1:T(8,128)} %copy.42), channel_id=1, source_target_pairs={{0,1},{1,2},{2,3},{4,5},{5,6},{6,7},{8,9},{9,10},{10,11},{12,13},{... | collective-permute-start | bytes 1044488 | tf_op jit(solution)/shard_map/ppermute | solution.py:31
  164.0 17.8 %collective-permute-start.9 = (f32[68,10,128]{2,0,1:T(8,128)}, f32[68,10,128]{2,0,1:T(8,128)S(1)}, u32[]{:S(2)}, u32[]{:S(2)}) collective-permute-start(f32[68,10,128]{2,0,1:T(8,128)} %copy.43), channel_id=1, source_target_pairs={{1,0},{2,1},{3,2},{5,4},{6,5},{7,6},{9,8},{10,9},{11,10},{13,12},{... | collective-permute-start | bytes 1044488 | tf_op jit(solution)/shard_map/ppermute | solution.py:31
  167.7 9.9 %all-to-all-start = ((f32[32,1,128]{2,1,0:T(1,128)}), f32[32,1,128]{2,1,0:T(1,128)S(1)}, u32[]{:S(2)}, u32[]{:S(2)}) async-start(f32[32,1,128]{2,1,0:T(1,128)} %broadcast_in_dim.11), calls=%async_computation | async-start | bytes 32768 | tf_op jit(solution)/shard_map/all_to_all | solution.py:365
where the time goes:
time: 263 us; the launch traced here: 259 us
  Pallas kernels  113 us (43%)
  local copies, waits for them, and re-layouts  45.8 us (17%)
  starting transfers between devices  34.9 us (13%)
  blocking collectives  29.8 us (11%)
  waiting for transfers between devices  28.6 us (11%)
  other arithmetic  5.92 us (2%)
    pallas_call x1, Pallas kernels, march(): pl.pallas_call(march_kernel, out_shape=(result, result), in_specs=[smem,...  76.2 us
    pallas_call x1, Pallas kernels, slab_energy(): pl.pallas_call(energy_kernel, grid=(loads,), out_shape=(jax.ShapeDtypeStr...  36.6 us
    all_to_all x1, blocking collectives, per_device(): lax.all_to_all(jnp.concatenate(chunks, axis=0), 'wide', split_axis=0, con...  29.8 us
    ppermute x10, starting transfers between devices, shift_from(): return lax.ppermute(part, axis, pairs)  29.7 us
    ppermute x10, waiting for transfers between devices, shift_from(): return lax.ppermute(part, axis, pairs)  27.4 us
    unnamed x25, local copies, waits for them, and re-layouts  12.5 us
    all_to_all x3, local copies, waits for them, and re-layouts, per_device(): lax.all_to_all(jnp.concatenate(chunks, axis=0), 'wide', split_axis=0, con...  6.7 us
    slice x7, local copies, waits for them, and re-layouts, shift_from(): part = lax.slice_in_dim(block, 0, width, axis=dim)  5.81 us
  transfers between devices with their start and end apart: 11, of which 4 were waited for; matrix products, arithmetic and copies ran while one was open for 8% of the time, Pallas kernels for 0%

commit v1 on v0

v1 whole, which is shorter than its diff:
```python
import functools

import jax
import jax.numpy as jnp
from jax import lax
from jax.experimental import pallas as pl
from jax.experimental.pallas import tpu as pltpu
from jax.sharding import PartitionSpec as P

BZ = 16
EXT_PASSES = 4
HJ_STEPS = 3
SHEAR = 0.384615
LAME = 0.576923
WENO_EPS = 1e-06
TIME_STEP = 0.3
TAP_SCALE = 1.0 / (48.0 * 48.0 * 8.0)
MARGIN = 3 * (HJ_STEPS - 1) + EXT_PASSES
SIDE = 16
MESH = pl.DeviceIdType.MESH
f32 = jnp.float32


def val_taps(a, b, c, d):
    return (a + d) + 23.0 * (b + c)


def der_taps(a, b, c, d):
    return (d - a) + 5.0 * (c - b)


def z_filters(u):
    size = u.shape[-1]
    rows = u.shape[0]
    lane = lax.broadcasted_iota(jnp.int32, (rows, 128), 1)
    count = size // 128
    tiles = [u[:, t * 128:(t + 1) * 128] for t in range(count)]
    zero = jnp.zeros((rows, 128), f32)
    up = [pltpu.roll(t, 1, 1) for t in tiles]
    one = [pltpu.roll(t, 127, 1) for t in tiles] + [zero]
    two = [pltpu.roll(t, 126, 1) for t in tiles] + [zero]
    vals, ders = [], []
    for t in range(count):
        before = jnp.where(lane == 0, up[t - 1] if t else zero, up[t])
        after = jnp.where(lane == 127, one[t + 1], one[t])
        second = jnp.where(lane >= 126, two[t + 1], two[t])
        vals.append(val_taps(before, tiles[t], after, second))
        ders.append(der_taps(before, tiles[t], after, second))
    return vals, ders


def minus_side(e0, e1, t0, t1, c1, c3, p, q6, r3):
    low = p * (e0 + (c1 + c1)) + q6 * (e0 + t1) + r3 * (t1 + c3)
    return low, (p + q6) + r3


def plus_side(e0, e1, t0, t1, c1, c3, r, q6, p3):
    high = r * (e1 + (c3 + c3)) + q6 * (e1 + t0) + p3 * (t0 + c1)
    return high, (r + q6) + p3


EPS = 0.75 * WENO_EPS


def both_sides(d6, e0, e1, s0, s2, q0, q1, q2, g0, g1, t0, t1):
    c1 = e0 + s0
    c3 = e1 - s2
    a = q0 + g0 * c1
    b = q1 + g0 * e1
    c = q2 + g1 * c3
    a, b, c = a * a, b * b, c * c
    p, q6, r = b * c, 6.0 * (a * c), a * b
    low, low_sum = minus_side(e0, e1, t0, t1, c1, c3, p, q6, 3.0 * r)
    high, high_sum = plus_side(e0, e1, t0, t1, c1, c3, r, q6, 3.0 * p)
    return d6 + low / low_sum, high / high_sum - d6


def godunov(minus, plus):
    up = jnp.maximum(jnp.maximum(minus, plus), 0.0)
    down = jnp.minimum(jnp.minimum(minus, plus), 0.0)
    return up * up, down * down


def along_lanes(mid):
    size = mid.shape[-1]
    lane = lax.broadcasted_iota(jnp.int32, mid.shape, 1)
    first, last = lane == 0, lane == size - 1

    def before(x, edge):
        return jnp.where(first, edge, pltpu.roll(x, 1, 1))

    def after(x, edge):
        return jnp.where(last, edge, pltpu.roll(x, size - 1, 1))

    d_low = mid - before(mid, 0.0)
    d_here = after(mid, 0.0) - mid
    e2 = d_here - d_low
    e1 = before(e2, mid)
    e0 = before(e1, 0.0)
    e3 = after(e2, mid)
    e4 = after(e3, 0.0)
    s = [e1 - e0, e2 - e1, e3 - e2, e4 - e3]
    q = [x * x + EPS for x in s]
    g = [0.75 * x for x in (e1, e2, e3)]
    t = [x + x for x in (e1, e2, e3)]
    c1, c3 = e1 + s[0], e2 - s[2]
    a, b, c = q[0] + g[0] * c1, q[1] + g[0] * e2, q[2] + g[1] * c3
    a, b, c = a * a, b * b, c * c
    low, low_sum = minus_side(e1, e2, t[0], t[1], c1, c3, b * c, 6.0 * (a * c), 3.0 * (a * b))
    c1, c3 = e2 + s[1], e3 - s[3]
    a, b, c = q[1] + g[1] * c1, q[2] + g[1] * e3, q[3] + g[2] * c3
    a, b, c = a * a, b * b, c * c
    high, high_sum = plus_side(e2, e3, t[1], t[2], c1, c3, a * b, 6.0 * (a * c), 3.0 * (b * c))
    return 6.0 * d_low + low / low_sum, high / high_sum - 6.0 * d_here


def along_rows(ref, z, start, count):
    u = [ref[z, pl.ds(start + k, count), :] for k in range(-2, 4)]
    d = [u[k + 1] - u[k] for k in range(5)]
    e = [d[k + 1] - d[k] for k in range(4)]
    s = [e[k + 1] - e[k] for k in range(3)]
    q = [x * x + EPS for x in s]
    return both_sides(
        6.0 * d[2], e[1], e[2], s[0], s[2], q[0], q[1], q[2], 0.75 * e[1], 0.75 * e[2], e[1] + e[1], e[2] + e[2]
    )


def along_planes(ref, gp, gm, z_lo, z_hi, at):
    u = [ref[z_lo - 3 + k, at, :] for k in range(5)]
    d = [u[k + 1] - u[k] for k in range(4)]
    e = [d[k + 1] - d[k] for k in range(3)]
    s = [e[k + 1] - e[k] for k in range(2)]
    q = [x * x + EPS for x in s]
    g = 0.75 * e[1]
    t = e[1] + e[1]
    newest, d_mid, d_new = u[4], d[2], d[3]
    behind = None
    for z in range(z_lo - 1, z_hi):
        plane = ref[z + 3, at, :]
        d_next = plane - newest
        e_next = d_next - d_new
        s_next = e_next - e[2]
        q_next = s_next * s_next + EPS
        g_next = 0.75 * e[2]
        t_next = e[2] + e[2]
        minus, plus = both_sides(
            6.0 * d_mid, e[1], e[2], s[0], s_next, q[0], q[1], q_next, g, g_next, t, t_next
        )
        if behind is not None:
            up, down = godunov(behind, plus)
            gp[z, at, :] = up
            gm[z, at, :] = down
        behind = minus
        newest, d_mid, d_new = plane, d_new, d_next
        e = [e[1], e[2], e_next]
        s = [s[1], s_next]
        q = [q[1], q_next]
        g, t = g_next, t_next


def block_flip(x):
    row = lax.broadcasted_iota(jnp.int32, (8, 128), 0)
    block = lax.broadcasted_iota(jnp.int32, (8, 128), 1) // 16
    far = pltpu.roll(pltpu.roll(x, 4, 0), 64, 1)
    x = jnp.where((row // 4) % 2 == (block // 4) % 2, x, far)
    for bit in (2, 1):
        row_bit, block_bit = (row // bit) % 2, (block // bit) % 2
        down = pltpu.roll(pltpu.roll(x, bit, 0), 128 - 16 * bit, 1)
        up = pltpu.roll(pltpu.roll(x, 8 - bit, 0), 16 * bit, 1)
        x = jnp.where(row_bit == block_bit, x, jnp.where(row_bit > block_bit, down, up))
    return x


def kernel(
    disp, mat, lev, next_ref, speed_ref,
    field, energy, stiff, packed, arrived, phi, peak_out, peak_in, peak_mid, peak_all,
    own_sem, x_send, x_recv, y_send, y_recv, c_send, c_recv, lev_sem, lev_send, lev_recv,
    a_sem, a_send, a_recv, f_send, f_recv, p_send, p_recv, n_send, n_recv,
    *, wide, narrow,
):
    i = lax.axis_index("wide")
    j = lax.axis_index("narrow")
    fields, size_x, size_y, size_z = disp.shape
    own_z, own_y, lanes = lev.shape
    deep, rows, _ = phi.shape
    tiles = size_z // 128
    groups = own_y // 8
    tail = size_y
    has = {(-1, 0): i > 0, (1, 0): i < wide - 1, (0, -1): j > 0, (0, 1): j < narrow - 1}
    for a in (-1, 1):
        for b in (-1, 1):
            has[(a, b)] = has[(a, 0)] & has[(0, b)]
    around = [(-1, 0), (1, 0), (0, -1), (0, 1), (-1, -1), (-1, 1), (1, -1), (1, 1)]

    def remote(src, dst, send, recv, w, n):
        return pltpu.make_async_remote_copy(
            src_ref=src, dst_ref=dst, send_sem=send, recv_sem=recv,
            device_id={"wide": w, "narrow": n}, device_id_type=MESH,
        )

    own_copies = [
        pltpu.make_async_copy(
            disp.at[3 * l:3 * l + 3], field.at[3 * l:3 * l + 3, 0:size_x, 0:size_y], own_sem.at[l]
        )
        for l in range(3)
    ]
    lev_copy = pltpu.make_async_copy(
        lev, phi.at[MARGIN:MARGIN + own_z, SIDE:SIDE + own_y], lev_sem
    )

    def plane_part(dx):
        if dx < 0:
            return slice(0, 2), slice(size_x, size_x + 2)
        if dx > 0:
            return slice(size_x - 1, size_x), slice(size_x + 2, size_x + 3)
        return slice(0, size_x), slice(0, size_x)

    def row_part(dy):
        if dy < 0:
            return slice(0, 2), slice(tail, tail + 2)
        return slice(size_y - 1, size_y), slice(tail + 7, tail + 8)

    def x_copy(dx, l, b):
        src, dst = plane_part(dx)
        at = slice(8 * b, 8 * b + 8)
        k = (dx + 1) // 2
        return remote(
            disp.at[3 * l:3 * l + 3, src, at], field.at[3 * l:3 * l + 3, dst, at],
            x_send.at[k, l, b], x_recv.at[k, l, b], i + dx, j,
        )

    def y_copy(dy, l):
        src, dst = row_part(dy)
        k = (dy + 1) // 2
        return remote(
            disp.at[3 * l:3 * l + 3, :, src], field.at[3 * l:3 * l + 3, 0:size_x, dst],
            y_send.at[k, l], y_recv.at[k, l], i, j + dy,
        )

    def c_copy(dx, dy):
        xs, xd = plane_part(dx)
        ys, yd = row_part(dy)
        k = (dx + 1) + (dy + 1) // 2
        return remote(
            disp.at[:, xs, ys], field.at[:, xd, yd], c_send.at[k], c_recv.at[k], i + dx, j + dy
        )

    def lev_part(step, size, width, before):
        if step < 0:
            return slice(0, width), slice(before + size, before + size + width)
        if step > 0:
            return slice(size - width, size), slice(before - width, before)
        return slice(0, size), slice(before, before + size)

    def lev_send_copy(k):
        dx, dy = around[k]
        zs, zd = lev_part(dx, own_z, MARGIN, MARGIN)
        ys, yd = lev_part(dy, own_y, MARGIN if lanes == 128 else SIDE, SIDE)
        return remote(lev.at[zs, ys], phi.at[zd, yd], lev_send.at[k], lev_recv.at[k], i + dx, j + dy)

    for copy in own_copies:
        copy.start()
    lev_copy.start()

    barrier = pltpu.get_barrier_semaphore()

    @pl.loop(1, wide)
    def _(k):
        pl.semaphore_signal(
            barrier, inc=1, device_id={"wide": (i + k) % wide, "narrow": j}, device_id_type=MESH
        )

    @pl.loop(1, narrow)
    def _(k):
        pl.semaphore_signal(
            barrier, inc=1, device_id={"wide": i, "narrow": (j + k) % narrow}, device_id_type=MESH
        )

    for dx, dy in around[4:]:
        @pl.when(has[(dx, dy)])
        def _(dx=dx, dy=dy):
            pl.semaphore_signal(
                barrier, inc=1, device_id={"wide": i + dx, "narrow": j + dy}, device_id_type=MESH
            )
    beside_x = jnp.where(i > 0, 1, 0) + jnp.where(i < wide - 1, 1, 0)
    beside_y = jnp.where(j > 0, 1, 0) + jnp.where(j < narrow - 1, 1, 0)
    pl.semaphore_wait(barrier, wide - 1 + narrow - 1 + beside_x * beside_y)

    for dy in (-1, 1):
        @pl.when(has[(0, dy)])
        def _(dy=dy):
            for l in range(3):
                y_copy(dy, l).start()
    for b in range(groups):
        for dx in (-1, 1):
            @pl.when(has[(dx, 0)])
            def _(dx=dx, b=b):
                for l in range(3):
                    x_copy(dx, l, b).start()
        if b == 0:
            for dx, dy in around[4:]:
                @pl.when(has[(dx, dy)])
                def _(dx=dx, dy=dy):
                    c_copy(dx, dy).start()
            for k in range(8):
                @pl.when(has[around[k]])
                def _(k=k):
                    lev_send_copy(k).start()

    for dx, planes in ((1, (size_x, size_x + 1)), (-1, (size_x + 2,))):
        @pl.when(jnp.logical_not(has[(dx, 0)]))
        def _(planes=planes):
            @pl.loop(0, fields)
            def _(f):
                for p in planes:
                    field[f, p] = jnp.zeros(field.shape[2:], f32)

    for dy, lo, hi in ((1, tail, tail + 2), (-1, tail + 7, tail + 8)):
        @pl.when(jnp.logical_not(has[(0, dy)]))
        def _(lo=lo, hi=hi):
            @pl.loop(0, fields)
            def _(f):
                for p in range(size_x + 3):
                    field[f, p, lo:hi, :] = jnp.zeros((hi - lo, size_z), f32)

    block = lax.broadcasted_iota(jnp.int32, (mat.shape[1], size_z), 0)
    column = lax.broadcasted_iota(jnp.int32, (mat.shape[1], size_z), 1) // BZ
    spread = jnp.where(block == column, 1.0, 0.0)
    solid = jnp.dot(mat[...].astype(f32), spread, preferred_element_type=f32)
    for t in range(tiles):
        stiff[t] = 0.2 + 0.8 * solid[:, t * 128:(t + 1) * 128]
        energy[t] = jnp.zeros(energy.shape[1:], f32)
    for b in range(groups):
        packed[b] = jnp.zeros(packed.shape[1:], f32)
    peak_out[...] = jnp.zeros(peak_out.shape, f32)

    def inside(z, lo, shape):
        here = i * own_z - MARGIN + z
        row = lax.broadcasted_iota(jnp.int32, shape, 0) + (lo + j * own_y - SIDE)
        end = narrow * own_y
        lowest = jnp.where((here >= 0) & (here < wide * own_z), 0, end)
        return (row >= lowest) & (row < end)

    def energy_phase(val, der, gp, gm):
        def filter_rows(f, p, at, spots):
            vals, ders = z_filters(field[f, p, at, :])
            for t in range(tiles):
                for spot in spots:
                    val[f, p, t, spot, :] = vals[t]
                    der[f, p, t, spot, :] = ders[t]

        tail_spots = (slice(0, 8), slice(8 + size_y, 16 + size_y))

        for l in range(3):
            own_copies[l].wait()

            @pl.loop(0, 3 * size_x)
            def _(k, l=l):
                filter_rows(
                    3 * l + k // size_x, k % size_x, slice(0, size_y), (slice(8, 8 + size_y),)
                )

        for dy in (-1, 1):
            @pl.when(has[(0, -dy)])
            def _(dy=dy):
                for l in range(3):
                    y_copy(dy, l).wait_recv()

        @pl.loop(0, fields)
        def _(f):
            for p in range(size_x):
                filter_rows(f, p, slice(tail, tail + 8), tail_spots)

        def march_planes(f, t, y, planes, out):
            held = []
            for n, p in enumerate(planes):
                v = [[val[f + c, p, t, pl.ds(y + 7 + k, 8), :] for k in range(4)] for c in range(3)]
                w = [[der[f + c, p, t, pl.ds(y + 7 + k, 8), :] for k in range(4)] for c in range(3)]
                vv = [val_taps(*x) for x in v]
                vd = [der_taps(*x) for x in v]
                dv = [val_taps(*x) for x in w]
                held.append((vv[0], vd[0], dv[0], vv[1], vd[1], vv[2], dv[2], dv[1] + vd[2]))
                if len(held) < 4:
                    continue
                line = list(zip(*held))
                held = held[1:]
                exx = der_taps(*line[0])
                eyy = val_taps(*line[4])
                ezz = val_taps(*line[6])
                exy = val_taps(*line[1]) + der_taps(*line[3])
                exz = val_taps(*line[2]) + der_taps(*line[5])
                eyz = val_taps(*line[7])
                trace = exx + eyy + ezz
                square = (exx * exx + eyy * eyy + ezz * ezz) + 0.5 * (exy * exy + exz * exz + eyz * eyz)
                density = (SHEAR * TAP_SCALE * TAP_SCALE) * square
                density = density + (0.5 * LAME * TAP_SCALE * TAP_SCALE) * (trace * trace)
                at = pl.ds(out[n - 3] * size_y + y, 8)
                energy[t, at, :] = energy[t, at, :] + density

        @pl.loop(0, 3 * tiles * groups)
        def _(k):
            y = pl.multiple_of((k % groups) * 8, 8)
            march_planes(
                3 * (k // (tiles * groups)), (k // groups) % tiles, y,
                list(range(size_x)), list(range(1, size_x - 2)),
            )

        lev_copy.wait()
        for k in range(8):
            dx, dy = around[k]

            @pl.when(has[(-dx, -dy)])
            def _(k=k):
                lev_send_copy(k).wait_recv()

        @pl.loop(0, deep)
        def _(z):
            for lo in range(0, rows, 16):
                at = pl.ds(lo, 16)
                held = phi[z, at, :]
                phi[z, at, :] = jnp.where(inside(z, lo, held.shape), held - 1.0, 0.0)

        z_lo, z_hi = MARGIN - 6, deep - (MARGIN - 6)

        def growth_piece(n):
            first_lo = SIDE - 8
            chunks = (own_y + 16) // 8
            span = z_hi - z_lo
            begin, end = z_lo + span * n // 3, z_lo + span * (n + 1) // 3

            @pl.loop(0, chunks)
            def _(c):
                at = pl.ds(pl.multiple_of(first_lo + 8 * c, 8), 8)
                along_planes(phi, gp, gm, begin, end, at)

            @pl.loop(begin, end)
            def _(z):
                plane_growth(phi, gp, gm, z, first_lo, chunks, first_lo, None)

        def take_halo(b):
            for dx in (-1, 1):
                @pl.when(has[(-dx, 0)])
                def _(dx=dx):
                    for l in range(3):
                        x_copy(dx, l, b).wait_recv()

            @pl.loop(0, fields)
            def _(f):
                for p in range(size_x, size_x + 3):
                    filter_rows(f, p, slice(8 * b, 8 * b + 8), (slice(8 * b + 8, 8 * b + 16),))

        def send_group(b):
            y = 8 * b

            @pl.loop(0, 3 * tiles)
            def _(k):
                march_planes(3 * (k // tiles), k % tiles, y, [size_x + 2, 0, 1, 2], [0])
                march_planes(
                    3 * (k // tiles), k % tiles, y,
                    [size_x - 3, size_x - 2, size_x - 1, size_x, size_x + 1], [size_x - 2, size_x - 1],
                )

            for t in range(tiles):
                parts = []
                for s in range(8):
                    at = pl.ds(y + s, size_x, stride=size_y)
                    parts.append(energy[t, at, :] * stiff[t, at, :])
                block = jnp.concatenate(parts, axis=0)
                top = jnp.max(block.reshape(block.shape[0] // 8, 8, 128), axis=0)
                peak_out[...] = jnp.maximum(peak_out[...], top)
                packed[b, MARGIN + 128 * t:MARGIN + 128 * (t + 1), :] = block.T

            pltpu.make_async_copy(
                packed.at[b, pl.ds(i * own_z, deep)], arrived.at[i, b + 2, pl.ds(0, deep)], a_sem.at[b]
            ).start()

            @pl.loop(1, wide)
            def _(k):
                w = (i + k) % wide
                remote(
                    packed.at[b, pl.ds(w * own_z, deep)], arrived.at[i, b + 2, pl.ds(0, deep)],
                    a_send.at[b, w], a_recv.at[b, i], w, j,
                ).start()

        for dx, dy in around[4:]:
            @pl.when(has[(-dx, -dy)])
            def _(dx=dx, dy=dy):
                c_copy(dx, dy).wait_recv()

        @pl.loop(0, fields)
        def _(f):
            for p in range(size_x, size_x + 3):
                filter_rows(f, p, slice(tail, tail + 8), tail_spots)

        take_halo(0)
        for b in range(groups):
            if b < groups - 1:
                take_halo(b + 1)
            send_group(b)
            if b < groups - 2:
                growth_piece(b)

        def wide_peak(k):
            w = (i + k) % wide
            return remote(peak_out, peak_in.at[i], p_send.at[w], p_recv.at[i], w, j)

        @pl.loop(1, wide)
        def _(k):
            wide_peak(k).start()

        def from_wide(k):
            s = (i + k) % wide
            return remote(peak_out, peak_in.at[s], p_send.at[s], p_recv.at[s], s, j)

        peak_mid[...] = peak_out[...]

        @pl.loop(1, wide)
        def _(k):
            from_wide(k).wait_recv()
            peak_mid[...] = jnp.maximum(peak_mid[...], peak_in[(i + k) % wide])

        def narrow_peak(k):
            n = (j + k) % narrow
            return remote(peak_mid, peak_all.at[j], n_send.at[n], n_recv.at[j], i, n)

        def from_narrow(k):
            s = (j + k) % narrow
            return remote(peak_mid, peak_all.at[s], n_send.at[s], n_recv.at[s], i, s)

        @pl.loop(1, narrow)
        def _(k):
            narrow_peak(k).start()

        for n in range(groups - 2, 3):
            growth_piece(n)

        def forward(b, s):
            near = -1 if b < 2 else 1
            slot = 6 + b if b < 2 else b - 2
            return near, remote(
                arrived.at[s, b + 2, pl.ds(0, deep)], arrived.at[s, slot, pl.ds(0, deep)], f_send.at[b, s], f_recv.at[b, s],
                i, j + near,
            )

        for b in range(groups):
            pltpu.make_async_copy(
                packed.at[b, pl.ds(i * own_z, deep)], arrived.at[i, b + 2, pl.ds(0, deep)], a_sem.at[b]
            ).wait()

            @pl.loop(0, wide)
            def _(k, b=b):
                s = (i + wide - k) % wide

                @pl.when(k > 0)
                def _():
                    remote(
                        packed.at[b, pl.ds(s * own_z, deep)], arrived.at[s, b + 2, pl.ds(0, deep)],
                        a_send.at[b, s], a_recv.at[b, s], s, j,
                    ).wait_recv()

                near = -1 if b < 2 else 1

                @pl.when(has[(0, near)])
                def _():
                    forward(b, s)[1].start()

        peak_all[j] = peak_mid[...]

        @pl.loop(1, narrow)
        def _(k):
            from_narrow(k).wait_recv()
            peak_all[j] = jnp.maximum(peak_all[j], peak_all[(j + k) % narrow])

        for b in range(groups):
            near = -1 if b < 2 else 1

            @pl.when(has[(0, -near)])
            def _(b=b):
                @pl.loop(0, wide)
                def _(s):
                    forward(b, s)[1].wait_recv()

        for b in range(groups):
            near = -1 if b < 2 else 1

            @pl.when(has[(0, near)])
            def _(b=b):
                @pl.loop(0, wide)
                def _(s):
                    forward(b, s)[1].wait_send()

            @pl.loop(1, wide)
            def _(k, b=b):
                w = (i + k) % wide
                remote(
                    packed.at[b, pl.ds(w * own_z, deep)], arrived.at[i, b + 2, pl.ds(0, deep)],
                    a_send.at[b, w], a_recv.at[b, i], w, j,
                ).wait_send()

        @pl.loop(1, wide)
        def _(k):
            wide_peak(k).wait_send()

        @pl.loop(1, narrow)
        def _(k):
            narrow_peak(k).wait_send()

        for dy in (-1, 1):
            @pl.when(has[(0, dy)])
            def _(dy=dy):
                for l in range(3):
                    y_copy(dy, l).wait_send()
        for dx in (-1, 1):
            @pl.when(has[(dx, 0)])
            def _(dx=dx):
                for l in range(3):
                    for b in range(groups):
                        x_copy(dx, l, b).wait_send()
        for dx, dy in around[4:]:
            @pl.when(has[(dx, dy)])
            def _(dx=dx, dy=dy):
                c_copy(dx, dy).wait_send()
        for k in range(8):
            @pl.when(has[around[k]])
            def _(k=k):
                lev_send_copy(k).wait_send()

    def plane_growth(source, gp, gm, z, start, chunks, rows_start, done):
        extra = 0 if rows_start == start else 1
        minus_parts, plus_parts = [], []
        for c in range(chunks + extra):
            minus, plus = along_rows(source, z, rows_start + 8 * c, 8)
            minus_parts.append(minus)
            plus_parts.append(plus)
        row = lax.broadcasted_iota(jnp.int32, (8, lanes), 0)
        for c in range(chunks):
            at = pl.ds(start + 8 * c, 8)
            if extra:
                low, here = minus_parts[c], minus_parts[c + 1]
                plus = plus_parts[c + 1]
            else:
                low, here = minus_parts[max(c - 1, 0)], minus_parts[c]
                plus = plus_parts[c]
            minus = jnp.where(row == 0, pltpu.roll(low, 1, 0), pltpu.roll(here, 1, 0))
            up_y, down_y = godunov(minus, plus)
            up_x, down_x = godunov(*along_lanes(source[z, at, :]))
            up = gp[z, at, :] + (up_y + up_x)
            down = gm[z, at, :] + (down_y + down_x)
            if done is None:
                gp[z, at, :] = jnp.sqrt(up)
                gm[z, at, :] = jnp.sqrt(down)
            else:
                done(z, at, c, up, down)

    def scoped(gp, gm):
        pl.run_scoped(
            lambda val, der: energy_phase(val, der, gp, gm),
            pltpu.VMEM((fields, size_x + 3, tiles, size_y + 16, 128), f32),
            pltpu.VMEM((fields, size_x + 3, tiles, size_y + 16, 128), f32),
        )
        pl.run_scoped(
            lambda *refs: march_phase(gp, gm, *refs),
            *[pltpu.VMEM(phi.shape, f32)] * 5,
        )

    def march_phase(gp, gm, psi, pull, keep, one, two):
        scale = jnp.max(peak_all[j]) + 1e-06
        flat = arrived.reshape(arrived.shape[0] * 8 * arrived.shape[2], 128)
        stride = 8 * arrived.shape[2]

        @pl.loop(0, deep)
        def _(z):
            for g in range(8):
                at = pl.ds(8 * g, 8)
                pieces = []
                for h in range(wide // 8):
                    first = h * 8 * stride + g * arrived.shape[2] + z
                    pieces.append(block_flip(flat[pl.ds(first, 8, stride=stride), :]))
                held = pieces[0] if len(pieces) == 1 else jnp.concatenate(pieces, axis=1)
                mask = inside(z, 8 * g, held.shape)
                velocity = jnp.where(mask, held / scale - 0.5, 0.0)
                level = phi[z, at, :] + 1.0
                weight = 1.0 / (1.0 + 4.0 * level * level)
                one[z, at, :] = velocity
                pull[z, at, :] = weight * velocity
                keep[z, at, :] = jnp.where(mask, (1.0 - weight) * (1.0 / 6.0), 0.0)

        source, target = one, two
        lane = lax.broadcasted_iota(jnp.int32, (8, lanes), 1)
        for step in range(EXT_PASSES):
            margin = MARGIN - 1 - step
            if step == 0:
                lo, chunks = SIDE - 12, (own_y + 24) // 8
            else:
                lo, chunks = SIDE - 8, (own_y + 16) // 8
            last = step == EXT_PASSES - 1

            def extend(z, source=source, target=target, lo=lo, chunks=chunks, last=last):
                for c in range(chunks):
                    start = lo + 8 * c
                    at = pl.ds(start, 8)
                    mid = source[z, at, :]
                    total = source[z - 1, at, :] + source[z + 1, at, :]
                    total = total + (source[z, pl.ds(start - 1, 8), :] + source[z, pl.ds(start + 1, 8), :])
                    low = jnp.where(lane == 0, 0.0, pltpu.roll(mid, 1, 1))
                    high = jnp.where(lane == lanes - 1, 0.0, pltpu.roll(mid, lanes - 1, 1))
                    value = pull[z, at, :] + keep[z, at, :] * (total + (low + high))
                    target[z, at, :] = value
                    if last:
                        growth = jnp.where(value > 0.0, gp[z, at, :], gm[z, at, :])
                        psi[z, at, :] = phi[z, at, :] - (TIME_STEP / 6.0) * (value * growth)

            pl.loop(step + 1, deep - step - 1)(extend)
            source, target = target, source
        speed = source

        source, target = psi, phi
        for step in range(1, HJ_STEPS):
            margin = 3 * (HJ_STEPS - 1 - step)
            final = step == HJ_STEPS - 1
            z_lo, z_hi = MARGIN - margin, MARGIN + own_z + margin
            if final:
                lo, chunks = SIDE, own_y // 8
            elif lanes == 128:
                lo, chunks = SIDE - 4, (own_y + 8) // 8
            else:
                lo, chunks = SIDE - 8, (own_y + 16) // 8
            unit = 8 if lo % 8 == 0 else 4

            @pl.loop(0, chunks)
            def _(c, source=source, lo=lo, unit=unit, z_lo=z_lo, z_hi=z_hi):
                along_planes(source, gp, gm, z_lo, z_hi, pl.ds(pl.multiple_of(lo + 8 * c, unit), 8))

            def done(z, at, c, up, down, source=source, target=target, final=final):
                rate = speed[z, at, :]
                growth = jnp.sqrt(jnp.where(rate > 0.0, up, down))
                value = source[z, at, :] - (TIME_STEP / 6.0) * (rate * growth)
                if final:
                    next_ref[z - MARGIN, pl.ds(8 * c, 8), :] = value + 1.0
                    speed_ref[z - MARGIN, pl.ds(8 * c, 8), :] = rate
                else:
                    target[z, at, :] = value

            rows_start = lo - 8 if final else lo

            @pl.loop(z_lo, z_hi)
            def _(z, source=source, lo=lo, chunks=chunks, rows_start=rows_start, done=done):
                plane_growth(source, gp, gm, z, lo, chunks, rows_start, done)

            source, target = target, source

    pl.run_scoped(scoped, pltpu.VMEM(phi.shape, f32), pltpu.VMEM(phi.shape, f32))


def per_device(displacement, material, level_set, wide, narrow):
    own_z, own_y, lanes = level_set.shape
    loads, comps, size_x, size_y, size_z = displacement.shape
    fields = loads * comps
    deep = own_z + 2 * MARGIN
    groups = own_y // 8
    tiles = size_z // 128
    padded = -(-(size_z + 2 * MARGIN) // 8) * 8
    result = jax.ShapeDtypeStruct((own_z, own_y, lanes), f32)
    dma = pltpu.SemaphoreType.DMA
    vmem = pl.BlockSpec(memory_space=pltpu.VMEM)
    hbm = pl.BlockSpec(memory_space=pl.ANY)
    return pl.pallas_call(
        functools.partial(kernel, wide=wide, narrow=narrow),
        out_shape=(result, result),
        in_specs=[hbm, vmem, hbm],
        out_specs=(vmem, vmem),
        scratch_shapes=[
            pltpu.VMEM((fields, size_x + 3, size_y + 8, size_z), f32),
            pltpu.VMEM((tiles, size_x * size_y, 128), f32),
            pltpu.VMEM((tiles, size_x * size_y, 128), f32),
            pltpu.VMEM((groups, padded, 128), f32),
            pltpu.VMEM((wide, 8, -(-deep // 8) * 8, 128), f32),
            pltpu.VMEM((deep, own_y + 2 * SIDE, lanes), f32),
            pltpu.VMEM((8, 128), f32),
            pltpu.VMEM((wide, 8, 128), f32),
            pltpu.VMEM((8, 128), f32),
            pltpu.VMEM((narrow, 8, 128), f32),
            dma((3,)), dma((2, 3, groups)), dma((2, 3, groups)), dma((2, 3)), dma((2, 3)), dma((4,)), dma((4,)),
            dma, dma((8,)), dma((8,)),
            dma((groups,)), dma((groups, wide)), dma((groups, wide)),
            dma((groups, wide)), dma((groups, wide)),
            dma((wide,)), dma((wide,)), dma((narrow,)), dma((narrow,)),
        ],
        compiler_params=pltpu.CompilerParams(
            vmem_limit_bytes=62 << 20, collective_id=0, has_side_effects=True
        ),
    )(
        displacement.reshape(fields, size_x, size_y, size_z),
        material.reshape(size_x * size_y, material.shape[2]),
        level_set,
    )


def solution(mesh):
    return jax.shard_map(
        functools.partial(per_device, wide=mesh.shape["wide"], narrow=mesh.shape["narrow"]),
        mesh=mesh,
        in_specs=(
            P(None, None, "wide", "narrow", None),
            P("wide", "narrow", None),
            P("wide", "narrow", None),
        ),
        out_specs=(P("wide", "narrow", None), P("wide", "narrow", None)),
        check_vma=False,
    )
```

time: 263 us -> 177 us (0.67); the launches traced: 259 us -> 176 us
  Pallas kernels: 113 us -> 170 us
  local copies, waits for them, and re-layouts: 45.8 us -> 5.89 us
  starting transfers between devices: 34.9 us -> 0 us
  blocking collectives: 29.8 us -> 0 us
  waiting for transfers between devices: 28.6 us -> 0 us
  other arithmetic: 5.92 us -> 0 us
    pallas_call x2 -> x1, Pallas kernels: 113 us -> 170 us  [per_device(): pl.pallas_call(functools.partial(kernel, wide=wide, narrow=narrow), out_s...]
    all_to_all x1 -> x0, blocking collectives: 29.8 us -> none  [per_device(): lax.all_to_all(jnp.concatenate(chunks, axis=0), 'wide', split_axis=0, con...]
    ppermute x10 -> x0, starting transfers between devices: 29.7 us -> none  [shift_from(): return lax.ppermute(part, axis, pairs)]
    ppermute x10 -> x0, waiting for transfers between devices: 27.4 us -> none  [shift_from(): return lax.ppermute(part, axis, pairs)]
    slice x18 -> x0, local copies, waits for them, and re-layouts: 11.6 us -> none  [the longest x7 5.81 us: shift_from(): part = lax.slice_in_dim(block, 0, width, axis=dim)]
    all_to_all x3 -> x0, local copies, waits for them, and re-layouts: 6.7 us -> none  [per_device(): lax.all_to_all(jnp.concatenate(chunks, axis=0), 'wide', split_axis=0, con...]
    unnamed x25 -> x3, local copies, waits for them, and re-layouts: 12.5 us -> 5.89 us
    all_to_all x1 -> x0, starting transfers between devices: 5.2 us -> none  [per_device(): lax.all_to_all(jnp.full((devices, 1, 128), own_peak), ('wide', 'narrow'),...]
  transfers between devices with their start and end apart: 11 -> 0, of which waited for: 4 -> 0; matrix products, arithmetic and copies ran while one was open for 8% -> 0% of each run, Pallas kernels for 0% -> 0%
where the time goes in v1:
time: 177 us; the launch traced here: 176 us
  Pallas kernels  170 us (96%)
  local copies, waits for them, and re-layouts  5.89 us (3%)
    pallas_call x1, Pallas kernels, per_device(): pl.pallas_call(functools.partial(kernel, wide=wide, narrow=narrow), out_s...  170 us
    unnamed x3, local copies, waits for them, and re-layouts  5.89 us

profile of v1, /device:TPU:17, one launch (start us, length us, event | category | flops | bytes accessed | tf_op | source)
XLA Modules:
  0.0 176.5 jit_solution(545972494808978468)
XLA Ops:
  0.6 1.8 copy.5
  2.4 170.0 %shard_map.50 = (f32[48,32,128]{2,1,0:T(8,128)}, f32[48,32,128]{2,1,0:T(8,128)}) custom-call(f32[9,16,32,384]{3,2,1,0:T(8,128)} %bitcast.2, s32[512,24]{1,0:T(8,128)} %bitcast.3, f32[48,32,128]{2,1,0:T(8,128)} %lev.1), custom_call_target="tpu_custom_call" | custom-call | tf_op jit(solution)/shard_map/pallas_call | solution.py:767
  172.4 2.1 %copy.8 = f32[48,32,128]{2,1,0:T(8,128)} copy(f32[48,32,128]{2,1,0:T(8,128)} %get-tuple-element.4) | data formatting | bytes 1572864
  174.4 2.1 %copy.9 = f32[48,32,128]{2,1,0:T(8,128)} copy(f32[48,32,128]{2,1,0:T(8,128)} %get-tuple-element.5) | data formatting | bytes 1572864

commit v2 on v1

--- a/solution.py
+++ b/solution.py
@@ -15,8 +15,9 @@
 WENO_EPS = 1e-06
 TIME_STEP = 0.3
 TAP_SCALE = 1.0 / (48.0 * 48.0 * 8.0)
-MARGIN = 3 * (HJ_STEPS - 1) + EXT_PASSES
-SIDE = 16
+MARGIN = EXT_PASSES
+SIDE = 8
+REACH = 3
 MESH = pl.DeviceIdType.MESH
 f32 = jnp.float32
 
@@ -84,21 +85,15 @@
 def along_lanes(mid):
     size = mid.shape[-1]
     lane = lax.broadcasted_iota(jnp.int32, mid.shape, 1)
-    first, last = lane == 0, lane == size - 1
-
-    def before(x, edge):
-        return jnp.where(first, edge, pltpu.roll(x, 1, 1))
-
-    def after(x, edge):
-        return jnp.where(last, edge, pltpu.roll(x, size - 1, 1))
-
-    d_low = mid - before(mid, 0.0)
-    d_here = after(mid, 0.0) - mid
-    e2 = d_here - d_low
-    e1 = before(e2, mid)
-    e0 = before(e1, 0.0)
-    e3 = after(e2, mid)
-    e4 = after(e3, 0.0)
+    u = []
+    for k in range(-3, 4):
+        if k == 0:
+            u.append(mid)
+            continue
+        moved = pltpu.roll(mid, (-k) % size, 1)
+        u.append(jnp.where(lane < -k if k < 0 else lane >= size - k, 0.0, moved))
+    d = [u[k + 1] - u[k] for k in range(6)]
+    e0, e1, e2, e3, e4 = [d[k + 1] - d[k] for k in range(5)]
     s = [e1 - e0, e2 - e1, e3 - e2, e4 - e3]
     q = [x * x + EPS for x in s]
     g = [0.75 * x for x in (e1, e2, e3)]
@@ -111,7 +106,7 @@
     a, b, c = q[1] + g[1] * c1, q[2] + g[1] * e3, q[3] + g[2] * c3
     a, b, c = a * a, b * b, c * c
     high, high_sum = plus_side(e2, e3, t[1], t[2], c1, c3, a * b, 6.0 * (a * c), 3.0 * (b * c))
-    return 6.0 * d_low + low / low_sum, high / high_sum - 6.0 * d_here
+    return 6.0 * d[2] + low / low_sum, high / high_sum - 6.0 * d[3]
 
 
 def along_rows(ref, z, start, count):
@@ -158,24 +153,29 @@
         g, t = g_next, t_next
 
 
-def block_flip(x):
+def block_flips(blocks):
     row = lax.broadcasted_iota(jnp.int32, (8, 128), 0)
-    block = lax.broadcasted_iota(jnp.int32, (8, 128), 1) // 16
-    far = pltpu.roll(pltpu.roll(x, 4, 0), 64, 1)
-    x = jnp.where((row // 4) % 2 == (block // 4) % 2, x, far)
+    part = lax.broadcasted_iota(jnp.int32, (8, 128), 1) // 16
+    far = [pltpu.roll(x, 4, 0) for x in blocks]
+    far = [pltpu.roll(x, 64, 1) for x in far]
+    same = (row // 4) % 2 == (part // 4) % 2
+    blocks = [jnp.where(same, x, y) for x, y in zip(blocks, far)]
     for bit in (2, 1):
-        row_bit, block_bit = (row // bit) % 2, (block // bit) % 2
-        down = pltpu.roll(pltpu.roll(x, bit, 0), 128 - 16 * bit, 1)
-        up = pltpu.roll(pltpu.roll(x, 8 - bit, 0), 16 * bit, 1)
-        x = jnp.where(row_bit == block_bit, x, jnp.where(row_bit > block_bit, down, up))
-    return x
+        row_bit, part_bit = (row // bit) % 2, (part // bit) % 2
+        down = [pltpu.roll(x, bit, 0) for x in blocks]
+        up = [pltpu.roll(x, 8 - bit, 0) for x in blocks]
+        down = [pltpu.roll(x, 128 - 16 * bit, 1) for x in down]
+        up = [pltpu.roll(x, 16 * bit, 1) for x in up]
+        same, below = row_bit == part_bit, row_bit > part_bit
+        blocks = [jnp.where(same, x, jnp.where(below, y, z)) for x, y, z in zip(blocks, down, up)]
+    return blocks
 
 
 def kernel(
     disp, mat, lev, next_ref, speed_ref,
-    field, energy, stiff, packed, arrived, phi, peak_out, peak_in, peak_mid, peak_all,
+    field, energy, stiff, packed, arrived, phi, psi, peak_out, peak_in, peak_mid, peak_all,
     own_sem, x_send, x_recv, y_send, y_recv, c_send, c_recv, lev_sem, lev_send, lev_recv,
-    a_sem, a_send, a_recv, f_send, f_recv, p_send, p_recv, n_send, n_recv,
+    a_sem, a_send, a_recv, f_send, f_recv, p_send, p_recv, n_send, n_recv, e_send, e_recv,
     *, wide, narrow,
 ):
     i = lax.axis_index("wide")
@@ -186,6 +186,8 @@
     tiles = size_z // 128
     groups = own_y // 8
     tail = size_y
+    reach_y = REACH if lanes == 128 else SIDE
+    slots = groups + 2
     has = {(-1, 0): i > 0, (1, 0): i < wide - 1, (0, -1): j > 0, (0, 1): j < narrow - 1}
     for a in (-1, 1):
         for b in (-1, 1):
@@ -254,9 +256,27 @@
 
     def lev_send_copy(k):
         dx, dy = around[k]
-        zs, zd = lev_part(dx, own_z, MARGIN, MARGIN)
-        ys, yd = lev_part(dy, own_y, MARGIN if lanes == 128 else SIDE, SIDE)
+        zs, zd = lev_part(dx, own_z, REACH, MARGIN)
+        ys, yd = lev_part(dy, own_y, reach_y, SIDE)
         return remote(lev.at[zs, ys], phi.at[zd, yd], lev_send.at[k], lev_recv.at[k], i + dx, j + dy)
+
+    def step_copy(n, ref, k):
+        dx, dy = around[k]
+        zs, zd = lev_part(dx, own_z, REACH, 0)
+        ys, yd = lev_part(dy, own_y, reach_y, 0)
+
+        def tile(z, y):
+            return ref.at[slice(z.start + MARGIN, z.stop + MARGIN), slice(y.start + SIDE, y.stop + SIDE)]
+
+        return remote(tile(zs, ys), tile(zd, yd), e_send.at[n, k], e_recv.at[n, k], i + dx, j + dy)
+
+    def step_do(n, ref, k, what):
+        dx, dy = around[k]
+        sign = -1 if what == "wait_recv" else 1
+
+        @pl.when(has[(sign * dx, sign * dy)])
+        def _():
+            getattr(step_copy(n, ref, k), what)()
 
     for copy in own_copies:
         copy.start()
@@ -326,13 +346,24 @@
     block = lax.broadcasted_iota(jnp.int32, (mat.shape[1], size_z), 0)
     column = lax.broadcasted_iota(jnp.int32, (mat.shape[1], size_z), 1) // BZ
     spread = jnp.where(block == column, 1.0, 0.0)
-    solid = jnp.dot(mat[...].astype(f32), spread, preferred_element_type=f32)
-    for t in range(tiles):
-        stiff[t] = 0.2 + 0.8 * solid[:, t * 128:(t + 1) * 128]
-        energy[t] = jnp.zeros(energy.shape[1:], f32)
+
+    @pl.loop(0, size_x)
+    def _(p):
+        solid = lax.dot_general(
+            mat[p].astype(f32), spread, (((0,), (0,)), ((), ())), preferred_element_type=f32
+        )
+        for t in range(tiles):
+            at = pl.ds(pl.multiple_of(p * size_y, 8), size_y)
+            stiff[t, at, :] = 0.2 + 0.8 * solid[:, t * 128:(t + 1) * 128]
+            energy[t, at, :] = jnp.zeros((size_y, 128), f32)
+
     for b in range(groups):
         packed[b] = jnp.zeros(packed.shape[1:], f32)
     peak_out[...] = jnp.zeros(peak_out.shape, f32)
+
+    @pl.loop(0, deep)
+    def _(z):
+        psi[z] = jnp.zeros(psi.shape[1:], f32)
 
     def inside(z, lo, shape):
         here = i * own_z - MARGIN + z
@@ -354,11 +385,13 @@
         for l in range(3):
             own_copies[l].wait()
 
-            @pl.loop(0, 3 * size_x)
+            @pl.loop(0, 3 * size_x // 2)
             def _(k, l=l):
-                filter_rows(
-                    3 * l + k // size_x, k % size_x, slice(0, size_y), (slice(8, 8 + size_y),)
-                )
+                for p in range(2):
+                    filter_rows(
+                        3 * l + (2 * k) // size_x, (2 * k) % size_x + p, slice(0, size_y),
+                        (slice(8, 8 + size_y),),
+                    )
 
         for dy in (-1, 1):
             @pl.when(has[(0, -dy)])
@@ -420,22 +453,14 @@
                 held = phi[z, at, :]
                 phi[z, at, :] = jnp.where(inside(z, lo, held.shape), held - 1.0, 0.0)
 
-        z_lo, z_hi = MARGIN - 6, deep - (MARGIN - 6)
-
         def growth_piece(n):
-            first_lo = SIDE - 8
-            chunks = (own_y + 16) // 8
-            span = z_hi - z_lo
-            begin, end = z_lo + span * n // 3, z_lo + span * (n + 1) // 3
-
-            @pl.loop(0, chunks)
+            begin, end = MARGIN + own_z * n // 3, MARGIN + own_z * (n + 1) // 3
+
+            @pl.loop(0, groups)
             def _(c):
-                at = pl.ds(pl.multiple_of(first_lo + 8 * c, 8), 8)
-                along_planes(phi, gp, gm, begin, end, at)
-
-            @pl.loop(begin, end)
-            def _(z):
-                plane_growth(phi, gp, gm, z, first_lo, chunks, first_lo, None)
+                along_planes(phi, gp, gm, begin, end, pl.ds(pl.multiple_of(SIDE + 8 * c, 8), 8))
+
+            plane_growth(phi, gp, gm, begin, end, None)
 
         def take_halo(b):
             for dx in (-1, 1):
@@ -471,14 +496,14 @@
                 packed[b, MARGIN + 128 * t:MARGIN + 128 * (t + 1), :] = block.T
 
             pltpu.make_async_copy(
-                packed.at[b, pl.ds(i * own_z, deep)], arrived.at[i, b + 2, pl.ds(0, deep)], a_sem.at[b]
+                packed.at[b, pl.ds(i * own_z, deep)], arrived.at[i, b + 1, pl.ds(0, deep)], a_sem.at[b]
             ).start()
 
             @pl.loop(1, wide)
             def _(k):
                 w = (i + k) % wide
                 remote(
-                    packed.at[b, pl.ds(w * own_z, deep)], arrived.at[i, b + 2, pl.ds(0, deep)],
+                    packed.at[b, pl.ds(w * own_z, deep)], arrived.at[i, b + 1, pl.ds(0, deep)],
                     a_send.at[b, w], a_recv.at[b, i], w, j,
                 ).start()
 
@@ -534,17 +559,18 @@
         for n in range(groups - 2, 3):
             growth_piece(n)
 
-        def forward(b, s):
-            near = -1 if b < 2 else 1
-            slot = 6 + b if b < 2 else b - 2
-            return near, remote(
-                arrived.at[s, b + 2, pl.ds(0, deep)], arrived.at[s, slot, pl.ds(0, deep)], f_send.at[b, s], f_recv.at[b, s],
-                i, j + near,
+        passed = ((0, -1, slots - 1), (groups - 1, 1, 0))
+
+        def forward(n, s):
+            b, near, slot = passed[n]
+            return remote(
+                arrived.at[s, b + 1, pl.ds(0, deep)], arrived.at[s, slot, pl.ds(0, deep)],
+                f_send.at[n, s], f_recv.at[n, s], i, j + near,
             )
 
         for b in range(groups):
             pltpu.make_async_copy(
-                packed.at[b, pl.ds(i * own_z, deep)], arrived.at[i, b + 2, pl.ds(0, deep)], a_sem.at[b]
+                packed.at[b, pl.ds(i * own_z, deep)], arrived.at[i, b + 1, pl.ds(0, deep)], a_sem.at[b]
             ).wait()
 
             @pl.loop(0, wide)
@@ -554,15 +580,15 @@
                 @pl.when(k > 0)
                 def _():
                     remote(
-                        packed.at[b, pl.ds(s * own_z, deep)], arrived.at[s, b + 2, pl.ds(0, deep)],
+                        packed.at[b, pl.ds(s * own_z, deep)], arrived.at[s, b + 1, pl.ds(0, deep)],
                         a_send.at[b, s], a_recv.at[b, s], s, j,
                     ).wait_recv()
 
-                near = -1 if b < 2 else 1
-
-                @pl.when(has[(0, near)])
-                def _():
-                    forward(b, s)[1].start()
+                for n in range(2):
+                    if passed[n][0] == b:
+                        @pl.when(has[(0, passed[n][1])])
+                        def _(n=n):
+                            forward(n, s).start()
 
         peak_all[j] = peak_mid[...]
 
@@ -571,29 +597,26 @@
             from_narrow(k).wait_recv()
             peak_all[j] = jnp.maximum(peak_all[j], peak_all[(j + k) % narrow])
 
-        for b in range(groups):
-            near = -1 if b < 2 else 1
-
-            @pl.when(has[(0, -near)])
-            def _(b=b):
+        for n in range(2):
+            @pl.when(has[(0, -passed[n][1])])
+            def _(n=n):
                 @pl.loop(0, wide)
                 def _(s):
-                    forward(b, s)[1].wait_recv()
-
-        for b in range(groups):
-            near = -1 if b < 2 else 1
-
-            @pl.when(has[(0, near)])
-            def _(b=b):
+                    forward(n, s).wait_recv()
+
+        for n in range(2):
+            @pl.when(has[(0, passed[n][1])])
+            def _(n=n):
                 @pl.loop(0, wide)
                 def _(s):
-                    forward(b, s)[1].wait_send()
-
+                    forward(n, s).wait_send()
+
+        for b in range(groups):
             @pl.loop(1, wide)
             def _(k, b=b):
                 w = (i + k) % wide
                 remote(
-                    packed.at[b, pl.ds(w * own_z, deep)], arrived.at[i, b + 2, pl.ds(0, deep)],
+                    packed.at[b, pl.ds(w * own_z, deep)], arrived.at[i, b + 1, pl.ds(0, deep)],
                     a_send.at[b, w], a_recv.at[b, i], w, j,
                 ).wait_send()
 
@@ -625,32 +648,34 @@
             def _(k=k):
                 lev_send_copy(k).wait_send()
 
-    def plane_growth(source, gp, gm, z, start, chunks, rows_start, done):
-        extra = 0 if rows_start == start else 1
-        minus_parts, plus_parts = [], []
-        for c in range(chunks + extra):
-            minus, plus = along_rows(source, z, rows_start + 8 * c, 8)
-            minus_parts.append(minus)
-            plus_parts.append(plus)
+    def plane_growth(source, gp, gm, begin, end, done):
+        if end <= begin:
+            return
         row = lax.broadcasted_iota(jnp.int32, (8, lanes), 0)
-        for c in range(chunks):
-            at = pl.ds(start + 8 * c, 8)
-            if extra:
-                low, here = minus_parts[c], minus_parts[c + 1]
-                plus = plus_parts[c + 1]
-            else:
-                low, here = minus_parts[max(c - 1, 0)], minus_parts[c]
-                plus = plus_parts[c]
-            minus = jnp.where(row == 0, pltpu.roll(low, 1, 0), pltpu.roll(here, 1, 0))
-            up_y, down_y = godunov(minus, plus)
-            up_x, down_x = godunov(*along_lanes(source[z, at, :]))
-            up = gp[z, at, :] + (up_y + up_x)
-            down = gm[z, at, :] + (down_y + down_x)
-            if done is None:
-                gp[z, at, :] = jnp.sqrt(up)
-                gm[z, at, :] = jnp.sqrt(down)
-            else:
-                done(z, at, c, up, down)
+        batch = 2 if (end - begin) % 2 == 0 else 1
+
+        def one_plane(z):
+            before, _ = along_rows(source, z, SIDE - 4, 8)
+            before = pltpu.roll(before, 5, 0)
+            for c in range(groups):
+                at = pl.ds(SIDE + 8 * c, 8)
+                here, plus = along_rows(source, z, SIDE + 8 * c, 8)
+                moved = pltpu.roll(here, 1, 0)
+                up_y, down_y = godunov(jnp.where(row == 0, before, moved), plus)
+                before = moved
+                up_x, down_x = godunov(*along_lanes(source[z, at, :]))
+                up = gp[z, at, :] + (up_y + up_x)
+                down = gm[z, at, :] + (down_y + down_x)
+                if done is None:
+                    gp[z, at, :] = jnp.sqrt(up)
+                    gm[z, at, :] = jnp.sqrt(down)
+                else:
+                    done(z, at, c, up, down)
+
+        @pl.loop(0, (end - begin) // batch)
+        def _(k):
+            for r in range(batch):
+                one_plane(begin + batch * k + r)
 
     def scoped(gp, gm):
         pl.run_scoped(
@@ -660,76 +685,111 @@
         )
         pl.run_scoped(
             lambda *refs: march_phase(gp, gm, *refs),
-            *[pltpu.VMEM(phi.shape, f32)] * 5,
-        )
-
-    def march_phase(gp, gm, psi, pull, keep, one, two):
+            *[pltpu.VMEM(phi.shape, f32)] * 4,
+        )
+
+    def most(count, options):
+        return next(n for n in options if count % n == 0)
+
+    def march_phase(gp, gm, pull, keep, one, two):
         scale = jnp.max(peak_all[j]) + 1e-06
-        flat = arrived.reshape(arrived.shape[0] * 8 * arrived.shape[2], 128)
-        stride = 8 * arrived.shape[2]
-
-        @pl.loop(0, deep)
-        def _(z):
-            for g in range(8):
-                at = pl.ds(8 * g, 8)
-                pieces = []
-                for h in range(wide // 8):
-                    first = h * 8 * stride + g * arrived.shape[2] + z
-                    pieces.append(block_flip(flat[pl.ds(first, 8, stride=stride), :]))
-                held = pieces[0] if len(pieces) == 1 else jnp.concatenate(pieces, axis=1)
-                mask = inside(z, 8 * g, held.shape)
-                velocity = jnp.where(mask, held / scale - 0.5, 0.0)
-                level = phi[z, at, :] + 1.0
-                weight = 1.0 / (1.0 + 4.0 * level * level)
-                one[z, at, :] = velocity
-                pull[z, at, :] = weight * velocity
-                keep[z, at, :] = jnp.where(mask, (1.0 - weight) * (1.0 / 6.0), 0.0)
-
+        flat = arrived.reshape(arrived.shape[0] * slots * arrived.shape[2], 128)
+        stride = slots * arrived.shape[2]
+        batch = most(deep, (2, 1))
+
+        @pl.loop(0, deep // batch)
+        def _(k):
+            raw = []
+            for r in range(batch):
+                for g in range(slots):
+                    for h in range(wide // 8):
+                        first = h * 8 * stride + g * arrived.shape[2] + batch * k + r
+                        raw.append(flat[pl.ds(first, 8, stride=stride), :])
+            raw = block_flips(raw)
+            for r in range(batch):
+                z = batch * k + r
+                for g in range(slots):
+                    at = pl.ds(8 * g, 8)
+                    pieces = [raw.pop(0) for _ in range(wide // 8)]
+                    held = pieces[0] if len(pieces) == 1 else jnp.concatenate(pieces, axis=1)
+                    mask = inside(z, 8 * g, held.shape)
+                    velocity = jnp.where(mask, held / scale - 0.5, 0.0)
+                    level = phi[z, at, :] + 1.0
+                    weight = 1.0 / (1.0 + 4.0 * level * level)
+                    one[z, at, :] = velocity
+                    pull[z, at, :] = weight * velocity
+                    keep[z, at, :] = jnp.where(mask, (1.0 - weight) * (1.0 / 6.0), 0.0)
+
+        top, bottom = MARGIN, MARGIN + own_z
+        edge = 6
         source, target = one, two
         lane = lax.broadcasted_iota(jnp.int32, (8, lanes), 1)
         for step in range(EXT_PASSES):
-            margin = MARGIN - 1 - step
-            if step == 0:
-                lo, chunks = SIDE - 12, (own_y + 24) // 8
-            else:
-                lo, chunks = SIDE - 8, (own_y + 16) // 8
             last = step == EXT_PASSES - 1
-
-            def extend(z, source=source, target=target, lo=lo, chunks=chunks, last=last):
-                for c in range(chunks):
-                    start = lo + 8 * c
+            lo, chunks = (SIDE, groups) if last else (SIDE - 4, groups + 1)
+
+            def extend(planes, source=source, target=target, lo=lo, chunks=chunks, last=last):
+                spots = [(z, lo + 8 * c) for z in planes for c in range(chunks)]
+                mids = [source[z, pl.ds(start, 8), :] for z, start in spots]
+                lows = [pltpu.roll(mid, 1, 1) for mid in mids]
+                highs = [pltpu.roll(mid, lanes - 1, 1) for mid in mids]
+                for (z, start), low, high in zip(spots, lows, highs):
                     at = pl.ds(start, 8)
-                    mid = source[z, at, :]
                     total = source[z - 1, at, :] + source[z + 1, at, :]
                     total = total + (source[z, pl.ds(start - 1, 8), :] + source[z, pl.ds(start + 1, 8), :])
-                    low = jnp.where(lane == 0, 0.0, pltpu.roll(mid, 1, 1))
-                    high = jnp.where(lane == lanes - 1, 0.0, pltpu.roll(mid, lanes - 1, 1))
+                    low = jnp.where(lane == 0, 0.0, low)
+                    high = jnp.where(lane == lanes - 1, 0.0, high)
                     value = pull[z, at, :] + keep[z, at, :] * (total + (low + high))
                     target[z, at, :] = value
                     if last:
                         growth = jnp.where(value > 0.0, gp[z, at, :], gm[z, at, :])
                         psi[z, at, :] = phi[z, at, :] - (TIME_STEP / 6.0) * (value * growth)
 
-            pl.loop(step + 1, deep - step - 1)(extend)
+            def extend_all(begin, end, extend=extend):
+                if end <= begin:
+                    return
+                size = most(end - begin, (6, 5, 4, 3, 2, 1))
+
+                @pl.loop(0, (end - begin) // size)
+                def _(k):
+                    extend([begin + size * k + r for r in range(size)])
+
+            if last:
+                extend_all(top, top + edge)
+                extend_all(bottom - edge, bottom)
+                step_do(0, psi, 0, "start")
+                extend_all(top + edge, bottom - edge)
+                step_do(0, psi, 1, "start")
+            else:
+                extend_all(step + 1, deep - step - 1)
             source, target = target, source
         speed = source
 
         source, target = psi, phi
         for step in range(1, HJ_STEPS):
-            margin = 3 * (HJ_STEPS - 1 - step)
             final = step == HJ_STEPS - 1
-            z_lo, z_hi = MARGIN - margin, MARGIN + own_z + margin
-            if final:
-                lo, chunks = SIDE, own_y // 8
-            elif lanes == 128:
-                lo, chunks = SIDE - 4, (own_y + 8) // 8
-            else:
-                lo, chunks = SIDE - 8, (own_y + 16) // 8
-            unit = 8 if lo % 8 == 0 else 4
-
-            @pl.loop(0, chunks)
-            def _(c, source=source, lo=lo, unit=unit, z_lo=z_lo, z_hi=z_hi):
-                along_planes(source, gp, gm, z_lo, z_hi, pl.ds(pl.multiple_of(lo + 8 * c, unit), 8))
+
+            def planes_of(begin, end, c, source=source):
+                along_planes(source, gp, gm, begin, end, pl.ds(pl.multiple_of(SIDE + 8 * c, 8), 8))
+
+            planes_of(top + REACH, bottom - REACH, 0)
+            for k in (2, 3):
+                step_do(step - 1, source, k, "start")
+
+            @pl.loop(1, groups)
+            def _(c, planes_of=planes_of):
+                planes_of(top + REACH, bottom - REACH, c)
+
+            for k in (0, 1):
+                step_do(step - 1, source, k, "wait_recv")
+
+            @pl.loop(0, groups)
+            def _(c, planes_of=planes_of):
+                planes_of(top, top + REACH, c)
+                planes_of(bottom - REACH, bottom, c)
+
+            for k in (2, 3):
+                step_do(step - 1, source, k, "wait_recv")
 
             def done(z, at, c, up, down, source=source, target=target, final=final):
                 rate = speed[z, at, :]
@@ -741,12 +801,16 @@
                 else:
                     target[z, at, :] = value
 
-            rows_start = lo - 8 if final else lo
-
-            @pl.loop(z_lo, z_hi)
-            def _(z, source=source, lo=lo, chunks=chunks, rows_start=rows_start, done=done):
-                plane_growth(source, gp, gm, z, lo, chunks, rows_start, done)
-
+            if final:
+                plane_growth(source, gp, gm, top, bottom, done)
+            else:
+                plane_growth(source, gp, gm, top, top + edge, done)
+                plane_growth(source, gp, gm, bottom - edge, bottom, done)
+                step_do(step, target, 0, "start")
+                plane_growth(source, gp, gm, top + edge, bottom - edge, done)
+                step_do(step, target, 1, "start")
+            for k in range(4):
+                step_do(step - 1, source, k, "wait_send")
             source, target = target, source
 
     pl.run_scoped(scoped, pltpu.VMEM(phi.shape, f32), pltpu.VMEM(phi.shape, f32))
@@ -774,7 +838,8 @@
             pltpu.VMEM((tiles, size_x * size_y, 128), f32),
             pltpu.VMEM((tiles, size_x * size_y, 128), f32),
             pltpu.VMEM((groups, padded, 128), f32),
-            pltpu.VMEM((wide, 8, -(-deep // 8) * 8, 128), f32),
+            pltpu.VMEM((wide, groups + 2, -(-deep // 8) * 8, 128), f32),
+            pltpu.VMEM((deep, own_y + 2 * SIDE, lanes), f32),
             pltpu.VMEM((deep, own_y + 2 * SIDE, lanes), f32),
             pltpu.VMEM((8, 128), f32),
             pltpu.VMEM((wide, 8, 128), f32),
@@ -783,15 +848,16 @@
             dma((3,)), dma((2, 3, groups)), dma((2, 3, groups)), dma((2, 3)), dma((2, 3)), dma((4,)), dma((4,)),
             dma, dma((8,)), dma((8,)),
             dma((groups,)), dma((groups, wide)), dma((groups, wide)),
-            dma((groups, wide)), dma((groups, wide)),
+            dma((2, wide)), dma((2, wide)),
             dma((wide,)), dma((wide,)), dma((narrow,)), dma((narrow,)),
+            dma((HJ_STEPS - 1, 4)), dma((HJ_STEPS - 1, 4)),
         ],
         compiler_params=pltpu.CompilerParams(
             vmem_limit_bytes=62 << 20, collective_id=0, has_side_effects=True
         ),
     )(
         displacement.reshape(fields, size_x, size_y, size_z),
-        material.reshape(size_x * size_y, material.shape[2]),
+        jnp.swapaxes(material, 1, 2),
         level_set,
     )
 

time: 177 us -> 107 us (0.60)
  Pallas kernels: 170 us -> 102 us
    pallas_call x1, Pallas kernels: 170 us -> 102 us  [per_device(): pl.pallas_call(functools.partial(kernel, wide=wide, narrow=narrow), out_s...]
    unnamed x3 -> x2, local copies, waits for them, and re-layouts: 5.89 us -> 4.13 us
where the time goes in v2:
time: 107 us
  Pallas kernels  102 us (95%)
  local copies, waits for them, and re-layouts  4.13 us (4%)
    pallas_call x1, Pallas kernels, per_device(): pl.pallas_call(functools.partial(kernel, wide=wide, narrow=narrow), out_s...  102 us
    unnamed x2, local copies, waits for them, and re-layouts  4.13 us

profile of v2, /device:TPU:17, one launch (start us, length us, event | category | flops | bytes accessed | tf_op | source)
XLA Modules:
  0.0 106.9 jit_solution(15874436507524290254)
XLA Ops:
  0.6 102.1 %shard_map.50 = (f32[48,32,128]{2,1,0:T(8,128)}, f32[48,32,128]{2,1,0:T(8,128)}) custom-call(f32[9,16,32,384]{3,2,1,0:T(8,128)} %bitcast.2, s32[16,24,32]{2,1,0:T(8,128)} %bitcast.3, f32[48,32,128]{2,1,0:T(8,128)} %lev.1), custom_call_target="tpu_custom_call" | custom-call | tf_op jit(solution)/shard_map/pallas_call | solution.py:831
  102.8 2.1 %copy.7 = f32[48,32,128]{2,1,0:T(8,128)} copy(f32[48,32,128]{2,1,0:T(8,128)} %get-tuple-element.4) | data formatting | bytes 1572864
  104.8 2.1 %copy.8 = f32[48,32,128]{2,1,0:T(8,128)} copy(f32[48,32,128]{2,1,0:T(8,128)} %get-tuple-element.5) | data formatting | bytes 1572864

commit v3 on v2

--- a/solution.py
+++ b/solution.py
@@ -173,7 +173,7 @@
 
 def kernel(
     disp, mat, lev, next_ref, speed_ref,
-    field, energy, stiff, packed, arrived, phi, psi, peak_out, peak_in, peak_mid, peak_all,
+    field, energy, stiff, packed, arrived, phi, psi, gp, gm, pull, keep, one, two, peak_out, peak_in, peak_mid, peak_all,
     own_sem, x_send, x_recv, y_send, y_recv, c_send, c_recv, lev_sem, lev_send, lev_recv,
     a_sem, a_send, a_recv, f_send, f_recv, p_send, p_recv, n_send, n_recv, e_send, e_recv,
     *, wide, narrow,
@@ -306,26 +306,31 @@
     beside_y = jnp.where(j > 0, 1, 0) + jnp.where(j < narrow - 1, 1, 0)
     pl.semaphore_wait(barrier, wide - 1 + narrow - 1 + beside_x * beside_y)
 
+    for k in range(8):
+        @pl.when(has[around[k]])
+        def _(k=k):
+            lev_send_copy(k).start()
     for dy in (-1, 1):
         @pl.when(has[(0, dy)])
         def _(dy=dy):
             for l in range(3):
                 y_copy(dy, l).start()
-    for b in range(groups):
+    for b in (0,):
         for dx in (-1, 1):
             @pl.when(has[(dx, 0)])
             def _(dx=dx, b=b):
                 for l in range(3):
                     x_copy(dx, l, b).start()
-        if b == 0:
-            for dx, dy in around[4:]:
-                @pl.when(has[(dx, dy)])
-                def _(dx=dx, dy=dy):
-                    c_copy(dx, dy).start()
-            for k in range(8):
-                @pl.when(has[around[k]])
-                def _(k=k):
-                    lev_send_copy(k).start()
+    for dx, dy in around[4:]:
+        @pl.when(has[(dx, dy)])
+        def _(dx=dx, dy=dy):
+            c_copy(dx, dy).start()
+    for b in (1,2,3,):
+        for dx in (-1, 1):
+            @pl.when(has[(dx, 0)])
+            def _(dx=dx, b=b):
+                for l in range(3):
+                    x_copy(dx, l, b).start()
 
     for dx, planes in ((1, (size_x, size_x + 1)), (-1, (size_x + 2,))):
         @pl.when(jnp.logical_not(has[(dx, 0)]))
@@ -347,15 +352,16 @@
     column = lax.broadcasted_iota(jnp.int32, (mat.shape[1], size_z), 1) // BZ
     spread = jnp.where(block == column, 1.0, 0.0)
 
-    @pl.loop(0, size_x)
-    def _(p):
-        solid = lax.dot_general(
-            mat[p].astype(f32), spread, (((0,), (0,)), ((), ())), preferred_element_type=f32
-        )
-        for t in range(tiles):
-            at = pl.ds(pl.multiple_of(p * size_y, 8), size_y)
-            stiff[t, at, :] = 0.2 + 0.8 * solid[:, t * 128:(t + 1) * 128]
-            energy[t, at, :] = jnp.zeros((size_y, 128), f32)
+    @pl.loop(0, size_x // 4)
+    def _(k):
+        for p in range(4):
+            solid = lax.dot_general(
+                mat[4 * k + p].astype(f32), spread, (((0,), (0,)), ((), ())), preferred_element_type=f32
+            )
+            for t in range(tiles):
+                at = pl.ds(pl.multiple_of((4 * k + p) * size_y, 8), size_y)
+                stiff[t, at, :] = 0.2 + 0.8 * solid[:, t * 128:(t + 1) * 128]
+                energy[t, at, :] = jnp.zeros((size_y, 128), f32)
 
     for b in range(groups):
         packed[b] = jnp.zeros(packed.shape[1:], f32)
@@ -372,7 +378,29 @@
         lowest = jnp.where((here >= 0) & (here < wide * own_z), 0, end)
         return (row >= lowest) & (row < end)
 
-    def energy_phase(val, der, gp, gm):
+    def most(count, options):
+        return next(n for n in options if count % n == 0)
+
+    flat = arrived.reshape(arrived.shape[0] * slots * arrived.shape[2], 128)
+    stride = slots * arrived.shape[2]
+
+    def unpack(slot):
+        batch = most(deep, (8, 7, 6, 5, 4, 3, 2, 1))
+
+        @pl.loop(0, deep // batch)
+        def _(k):
+            raw = []
+            for r in range(batch):
+                for h in range(wide // 8):
+                    first = h * 8 * stride + slot * arrived.shape[2] + batch * k + r
+                    raw.append(flat[pl.ds(first, 8, stride=stride), :])
+            raw = block_flips(raw)
+            for r in range(batch):
+                pieces = [raw.pop(0) for _ in range(wide // 8)]
+                held = pieces[0] if len(pieces) == 1 else jnp.concatenate(pieces, axis=1)
+                one[batch * k + r, pl.ds(8 * slot, 8), :] = held
+
+    def energy_phase(val, der):
         def filter_rows(f, p, at, spots):
             vals, ders = z_filters(field[f, p, at, :])
             for t in range(tiles):
@@ -451,7 +479,11 @@
             for lo in range(0, rows, 16):
                 at = pl.ds(lo, 16)
                 held = phi[z, at, :]
-                phi[z, at, :] = jnp.where(inside(z, lo, held.shape), held - 1.0, 0.0)
+                mask = inside(z, lo, held.shape)
+                weight = 1.0 / (1.0 + 4.0 * held * held)
+                pull[z, at, :] = weight
+                keep[z, at, :] = jnp.where(mask, (1.0 - weight) * (1.0 / 6.0), 0.0)
+                phi[z, at, :] = jnp.where(mask, held - 1.0, 0.0)
 
         def growth_piece(n):
             begin, end = MARGIN + own_z * n // 3, MARGIN + own_z * (n + 1) // 3
@@ -522,7 +554,7 @@
             if b < groups - 1:
                 take_halo(b + 1)
             send_group(b)
-            if b < groups - 2:
+            if b < groups - 1:
                 growth_piece(b)
 
         def wide_peak(k):
@@ -556,8 +588,6 @@
         def _(k):
             narrow_peak(k).start()
 
-        for n in range(groups - 2, 3):
-            growth_piece(n)
 
         passed = ((0, -1, slots - 1), (groups - 1, 1, 0))
 
@@ -590,6 +620,8 @@
                         def _(n=n):
                             forward(n, s).start()
 
+            unpack(b + 1)
+
         peak_all[j] = peak_mid[...]
 
         @pl.loop(1, narrow)
@@ -603,6 +635,8 @@
                 @pl.loop(0, wide)
                 def _(s):
                     forward(n, s).wait_recv()
+
+            unpack(passed[n][2])
 
         for n in range(2):
             @pl.when(has[(0, passed[n][1])])
@@ -652,7 +686,7 @@
         if end <= begin:
             return
         row = lax.broadcasted_iota(jnp.int32, (8, lanes), 0)
-        batch = 2 if (end - begin) % 2 == 0 else 1
+        batch = most(end - begin, (3, 2, 1)) if end - begin < 8 else most(end - begin, (4, 3, 2, 1))
 
         def one_plane(z):
             before, _ = along_rows(source, z, SIDE - 4, 8)
@@ -677,48 +711,18 @@
             for r in range(batch):
                 one_plane(begin + batch * k + r)
 
-    def scoped(gp, gm):
-        pl.run_scoped(
-            lambda val, der: energy_phase(val, der, gp, gm),
-            pltpu.VMEM((fields, size_x + 3, tiles, size_y + 16, 128), f32),
-            pltpu.VMEM((fields, size_x + 3, tiles, size_y + 16, 128), f32),
-        )
-        pl.run_scoped(
-            lambda *refs: march_phase(gp, gm, *refs),
-            *[pltpu.VMEM(phi.shape, f32)] * 4,
-        )
-
-    def most(count, options):
-        return next(n for n in options if count % n == 0)
-
-    def march_phase(gp, gm, pull, keep, one, two):
+
+    def march_phase():
         scale = jnp.max(peak_all[j]) + 1e-06
-        flat = arrived.reshape(arrived.shape[0] * slots * arrived.shape[2], 128)
-        stride = slots * arrived.shape[2]
-        batch = most(deep, (2, 1))
-
-        @pl.loop(0, deep // batch)
-        def _(k):
-            raw = []
-            for r in range(batch):
-                for g in range(slots):
-                    for h in range(wide // 8):
-                        first = h * 8 * stride + g * arrived.shape[2] + batch * k + r
-                        raw.append(flat[pl.ds(first, 8, stride=stride), :])
-            raw = block_flips(raw)
-            for r in range(batch):
-                z = batch * k + r
-                for g in range(slots):
-                    at = pl.ds(8 * g, 8)
-                    pieces = [raw.pop(0) for _ in range(wide // 8)]
-                    held = pieces[0] if len(pieces) == 1 else jnp.concatenate(pieces, axis=1)
-                    mask = inside(z, 8 * g, held.shape)
-                    velocity = jnp.where(mask, held / scale - 0.5, 0.0)
-                    level = phi[z, at, :] + 1.0
-                    weight = 1.0 / (1.0 + 4.0 * level * level)
-                    one[z, at, :] = velocity
-                    pull[z, at, :] = weight * velocity
-                    keep[z, at, :] = jnp.where(mask, (1.0 - weight) * (1.0 / 6.0), 0.0)
+
+        @pl.loop(0, deep)
+        def _(z):
+            for lo in range(0, rows, 16):
+                at = pl.ds(lo, 16)
+                held = one[z, at, :]
+                velocity = jnp.where(inside(z, lo, held.shape), held / scale - 0.5, 0.0)
+                one[z, at, :] = velocity
+                pull[z, at, :] = pull[z, at, :] * velocity
 
         top, bottom = MARGIN, MARGIN + own_z
         edge = 6
@@ -796,7 +800,7 @@
                 growth = jnp.sqrt(jnp.where(rate > 0.0, up, down))
                 value = source[z, at, :] - (TIME_STEP / 6.0) * (rate * growth)
                 if final:
-                    next_ref[z - MARGIN, pl.ds(8 * c, 8), :] = value + 1.0
+                    next_ref[z - MARGIN, pl.ds(8 * c, 8), :] = value
                     speed_ref[z - MARGIN, pl.ds(8 * c, 8), :] = rate
                 else:
                     target[z, at, :] = value
@@ -813,7 +817,12 @@
                 step_do(step - 1, source, k, "wait_send")
             source, target = target, source
 
-    pl.run_scoped(scoped, pltpu.VMEM(phi.shape, f32), pltpu.VMEM(phi.shape, f32))
+    pl.run_scoped(
+        energy_phase,
+        pltpu.VMEM((fields, size_x + 3, tiles, size_y + 16, 128), f32),
+        pltpu.VMEM((fields, size_x + 3, tiles, size_y + 16, 128), f32),
+    )
+    march_phase()
 
 
 def per_device(displacement, material, level_set, wide, narrow):
@@ -828,7 +837,7 @@
     dma = pltpu.SemaphoreType.DMA
     vmem = pl.BlockSpec(memory_space=pltpu.VMEM)
     hbm = pl.BlockSpec(memory_space=pl.ANY)
-    return pl.pallas_call(
+    level, speed = pl.pallas_call(
         functools.partial(kernel, wide=wide, narrow=narrow),
         out_shape=(result, result),
         in_specs=[hbm, vmem, hbm],
@@ -839,8 +848,7 @@
             pltpu.VMEM((tiles, size_x * size_y, 128), f32),
             pltpu.VMEM((groups, padded, 128), f32),
             pltpu.VMEM((wide, groups + 2, -(-deep // 8) * 8, 128), f32),
-            pltpu.VMEM((deep, own_y + 2 * SIDE, lanes), f32),
-            pltpu.VMEM((deep, own_y + 2 * SIDE, lanes), f32),
+            *[pltpu.VMEM((deep, own_y + 2 * SIDE, lanes), f32)] * 8,
             pltpu.VMEM((8, 128), f32),
             pltpu.VMEM((wide, 8, 128), f32),
             pltpu.VMEM((8, 128), f32),
@@ -861,6 +869,17 @@
         level_set,
     )
 
+    def finish(level_in, speed_in, level_out, speed_out):
+        level_out[...] = level_in[...] + 1.0
+        speed_out[...] = speed_in[...]
+
+    return pl.pallas_call(
+        finish,
+        out_shape=(result, result),
+        in_specs=[vmem, vmem],
+        out_specs=(vmem, vmem),
+    )(level, speed)
+
 
 def solution(mesh):
     return jax.shard_map(

time: 107 us -> 102 us (0.953); the launches traced: 107 us -> 101 us
  local copies, waits for them, and re-layouts: 4.13 us -> 0 us
  Pallas kernels: 102 us -> 99.9 us
    pallas_call x1, Pallas kernels: 102 us -> 97.3 us  [per_device(): pl.pallas_call(functools.partial(kernel, wide=wide, narrow=narrow), out_s...]
    unnamed x2 -> x0, local copies, waits for them, and re-layouts: 4.13 us -> none
    pallas_call x0 -> x1, Pallas kernels: none -> 2.56 us  [per_device(): pl.pallas_call(finish, out_shape=(result, result), in_specs=[vmem, vmem],...]
where the time goes in v3:
time: 102 us; the launch traced here: 101 us
  Pallas kernels  99.9 us (98%)
    pallas_call x1, Pallas kernels, per_device(): pl.pallas_call(functools.partial(kernel, wide=wide, narrow=narrow), out_s...  97.3 us
    pallas_call x1, Pallas kernels, per_device(): pl.pallas_call(finish, out_shape=(result, result), in_specs=[vmem, vmem],...  2.56 us

profile of v3, /device:TPU:17, one launch (start us, length us, event | category | flops | bytes accessed | tf_op | source)
XLA Modules:
  0.0 100.5 jit_solution(1699680376631846683)
XLA Ops:
  0.6 97.3 %shard_map.50 = (f32[48,32,128]{2,1,0:T(8,128)}, f32[48,32,128]{2,1,0:T(8,128)}) custom-call(f32[9,16,32,384]{3,2,1,0:T(8,128)} %bitcast.2, s32[16,24,32]{2,1,0:T(8,128)} %bitcast.3, f32[48,32,128]{2,1,0:T(8,128)} %lev.1), custom_call_target="tpu_custom_call" | custom-call | tf_op jit(solution)/shard_map/pallas_call | solution.py:840
  97.9 2.6 %shard_map.51 = (f32[48,32,128]{2,1,0:T(8,128)}, f32[48,32,128]{2,1,0:T(8,128)}) custom-call(f32[48,32,128]{2,1,0:T(8,128)} %get-tuple-element.4.level_in, f32[48,32,128]{2,1,0:T(8,128)} %get-tuple-element.5.speed_in), custom_call_target="tpu_custom_call" | custom-call | tf_op jit(solution)/shard_map/pallas_call | solution.py:876

commit v4 on v3

--- a/solution.py
+++ b/solution.py
@@ -686,7 +686,7 @@
         if end <= begin:
             return
         row = lax.broadcasted_iota(jnp.int32, (8, lanes), 0)
-        batch = most(end - begin, (3, 2, 1)) if end - begin < 8 else most(end - begin, (4, 3, 2, 1))
+        batch = most(end - begin, (6, 4, 3, 2, 1))
 
         def one_plane(z):
             before, _ = along_rows(source, z, SIDE - 4, 8)
@@ -752,7 +752,7 @@
             def extend_all(begin, end, extend=extend):
                 if end <= begin:
                     return
-                size = most(end - begin, (6, 5, 4, 3, 2, 1))
+                size = most(end - begin, (9, 13, 10, 8, 6, 5, 4, 3, 2, 1))
 
                 @pl.loop(0, (end - begin) // size)
                 def _(k):

time: 102 us -> 100 us (0.980)
  Pallas kernels: 99.9 us -> 98.3 us
    pallas_call x1, Pallas kernels: 97.3 us -> 95.7 us  [per_device(): pl.pallas_call(functools.partial(kernel, wide=wide, narrow=narrow), out_s...]
where the time goes in v4:
time: 100 us; the launch traced here: 98.9 us
  Pallas kernels  98.3 us (98%)
    pallas_call x1, Pallas kernels, per_device(): pl.pallas_call(functools.partial(kernel, wide=wide, narrow=narrow), out_s...  95.7 us
    pallas_call x1, Pallas kernels, per_device(): pl.pallas_call(finish, out_shape=(result, result), in_specs=[vmem, vmem],...  2.56 us

profile of v4, /device:TPU:17, one launch (start us, length us, event | category | flops | bytes accessed | tf_op | source)
XLA Modules:
  0.0 98.9 jit_solution(4641691629613236004)
XLA Ops:
  0.6 95.7 %shard_map.50 = (f32[48,32,128]{2,1,0:T(8,128)}, f32[48,32,128]{2,1,0:T(8,128)}) custom-call(f32[9,16,32,384]{3,2,1,0:T(8,128)} %bitcast.2, s32[16,24,32]{2,1,0:T(8,128)} %bitcast.3, f32[48,32,128]{2,1,0:T(8,128)} %lev.1), custom_call_target="tpu_custom_call" | custom-call | tf_op jit(solution)/shard_map/pallas_call | solution.py:840
  96.4 2.6 %shard_map.51 = (f32[48,32,128]{2,1,0:T(8,128)}, f32[48,32,128]{2,1,0:T(8,128)}) custom-call(f32[48,32,128]{2,1,0:T(8,128)} %get-tuple-element.4.level_in, f32[48,32,128]{2,1,0:T(8,128)} %get-tuple-element.5.speed_in), custom_call_target="tpu_custom_call" | custom-call | tf_op jit(solution)/shard_map/pallas_call | solution.py:876
